TPU v7x, 128 devices: a whole 4x4x4 slice. The times are simulated.
128 devices in a mesh: row: 8 (over y, core), col: 16 (over x, z).
Axes of the slice: x: 4, y: 4, z: 4, core: 2. Of those that a mesh axis runs over, the one named last changes fastest.
Arguments:
- strip_columns: float32 [4096, 32, 256], P(('row', 'col')), may hold values from -0.0048828125 to 0.0048828125
- tile_columns: float32 [4096, 4, 32, 256], P(('row', 'col')), may hold values from -6 to 6
- barrier_weights: float32 [4096, 32], P(('row', 'col')), may hold values from 0.01 to 100
- column_counts: int32 [4096], P(('row', 'col')), may hold values from 1 to 32
- tile_lists: int32 [4096, 4], P(('row', 'col')), may hold values from 0 to 127, all different within a row; in each aligned block of 32 rows (0 to 31, 32 to 63, ...) at most 2 rows name the same one
Outputs:
- panel_factor: float32 [256, 256], replicated
- strip_update: float32 [256, 32768], P(None, ('row', 'col'))
Inputs may be any that keep to these rules, and one draw needn't show every extreme that they name: `tile_lists`: each block lists 4 different column tiles; among the 32 blocks of one device no tile is listed more than 2 times, and in some device one tile is listed exactly 2 times.
All inputs are finite; a program needn't handle non-finite values.
Results may differ from a plain program's by a relative error of at most 0.0001.
Values sent between devices are 32-bit elements; how exact they have to be, the bound alone decides.
A program may use at most 192 MiB of HBM per device.

v0:
```python
import jax
import jax.numpy as jnp
from jax import lax
from jax.sharding import PartitionSpec as P


def per_device(strip_columns, tile_columns, barrier_weights, column_counts, tile_lists):
    highest = lax.Precision.HIGHEST
    blocks, block_width, strip_rows = strip_columns.shape
    touched = tile_columns.shape[1]
    own_width = tile_columns.shape[3]
    devices = lax.axis_size(("row", "col"))
    live_mask = jnp.arange(block_width, dtype=jnp.int32)[None, :] < column_counts[:, None]
    live_weight = jnp.where(live_mask, barrier_weights, 0.0)
    scaled = strip_columns * live_weight[:, :, None]
    local_diagonal = lax.dot_general(
        scaled, strip_columns, (((0, 1), (0, 1)), ((), ())), precision=highest
    )
    diagonal_block = lax.psum(local_diagonal, ("row", "col"))
    item_count = blocks * touched
    capacity = max(2, 2 * item_count // devices)
    targets = tile_lists.reshape(item_count)
    one_hot = (targets[:, None] == jnp.arange(devices, dtype=jnp.int32)[None, :]).astype(jnp.int32)
    earlier = jnp.cumsum(one_hot, axis=0) - one_hot
    ranked = jnp.sum(earlier * one_hot, axis=1)
    slot_index = targets * capacity + ranked
    slot_item = (
        jnp.full((devices * capacity,), -1, jnp.int32)
        .at[slot_index]
        .set(jnp.arange(item_count, dtype=jnp.int32))
    )
    filled = slot_item >= 0
    picked = jnp.maximum(slot_item, 0)
    send_strip = scaled[picked // touched]
    send_tile = tile_columns.reshape(item_count, block_width, own_width)[picked]
    outgoing = jnp.where(
        filled[:, None, None], jnp.concatenate([send_strip, send_tile], axis=2), 0.0
    )
    incoming = lax.all_to_all(outgoing, ("row", "col"), split_axis=0, concat_axis=0, tiled=True)
    tile_sum = lax.dot_general(
        incoming[:, :, :strip_rows],
        incoming[:, :, strip_rows:],
        (((0, 1), (0, 1)), ((), ())),
        precision=highest,
    )
    panel_factor = jnp.linalg.cholesky(diagonal_block)
    strip_update = jax.scipy.linalg.solve_triangular(panel_factor, tile_sum, lower=True)
    return (panel_factor, strip_update)


def solution(mesh):
    return jax.shard_map(
        per_device,
        mesh=mesh,
        in_specs=(
            P(("row", "col"), None, None),
            P(("row", "col"), None, None, None),
            P(("row", "col"), None),
            P(("row", "col")),
            P(("row", "col"), None),
        ),
        out_specs=(P(), P(None, ("row", "col"))),
        check_vma=False,
    )
```

profile of v0, /device:TPU:0, one launch (start us, length us, event | category | flops | bytes accessed | tf_op | source)
XLA Modules:
  0.0 456.1 jit_solution(12866232470006165996)
XLA Ops:
  7.2 0.7 broadcast_multiply_fusion.2
  7.8 0.8 copy.22
  8.6 0.1 copy.21
  8.7 0.1 mul.31
  8.8 0.1 eq.15
  8.9 0.1 fusion.17
  9.0 0.2 reduce_window_sum.11
  9.2 0.2 select_reduce_fusion
  9.4 1.0 scatter_custom_fusion
  10.4 0.8 fusion.18
  11.2 0.0 copy-start
  11.2 6.6 %gather_fusion.1 = f32[256,32,256]{2,1,0:T(8,128)} fusion(f32[128,32,256]{2,1,0:T(8,128)} %bitcast.43, s32[1024]{0:T(1024)S(1)} %get-tuple-element.34), kind=kCustom, calls=%fused_computation.1 | custom fusion | bytes 16778240 | tf_op jit(solution)/shard_map/gather | solution.py:35
  17.8 0.0 copy-done
  17.8 0.2 broadcast_multiply_fusion
  18.0 4.3 gather_fusion
  22.3 11.6 %maximum_select_fusion = f32[256,32,512]{2,1,0:T(8,128)} fusion(f32[256,32,256]{2,1,0:T(8,128)} %gather_fusion.1, f32[256,32,256]{2,1,0:T(8,128)} %gather_fusion, pred[256]{0:T(512)(128)(4,1)S(1)} %broadcast_compare_fusion), kind=kLoop, calls=%fused_computation.5 | loop fusion | flops 8388608 | bytes 33554688 | tf_op jit(solution)/shard_map/jit(_where)/select_n | solution.py:36
  34.0 11.7 %all-to-all-start = ((f32[256,32,512]{2,1,0:T(8,128)}), f32[256,32,512]{2,1,0:T(8,128)}, u32[]{:S(2)}, u32[]{:S(2)}) async-start(f32[256,32,512]{2,1,0:T(8,128)} %maximum_select_fusion), calls=%async_computation | async-start | bytes 33554432 | tf_op jit(solution)/shard_map/all_to_all | solution.py:39
  45.7 0.4 all-reduce.3.cloned.1.call-start
  46.1 2.7 convolution_bitcast_fusion
  48.8 0.0 all-reduce.3.cloned.1.call-update
  48.8 297.0 %all-reduce.3.cloned.1.call-done = f32[256,256]{0,1:T(8,128)} async-done(((f32[256,256]{0,1:T(8,128)}), f32[256,256]{0,1:T(8,128)}) %all-reduce.3.cloned.1.call-update) | async-done | bytes 262160 | tf_op jit(solution)/shard_map/psum | solution.py:19
  345.9 1.1 copy.20
  346.9 1.0 fusion.8
  347.9 11.7 %cholesky.51 = f32[128,128]{1,0:T(8,128)S(1)} custom-call(f32[128,128]{1,0:T(8,128)S(1)} %cholesky.121), custom_call_target="Cholesky" | custom-call | tf_op jit(solution)/shard_map/jit(cholesky)/cholesky | solution.py:46
  359.7 9.8 %custom-call.15 = f32[1,128,128]{1,2,0:T(8,128)S(1)} custom-call(f32[1,128,128]{2,1,0:T(8,128)S(1)} %get-tuple-element.27), custom_call_target="InvertDiagBlocksLowerTriangular" | custom-call | tf_op jit(solution)/shard_map/jit(cholesky)/cholesky | solution.py:46
  369.5 0.2 constant_dynamic-update-slice_fusion.1
  369.7 0.3 convolution_subtract_fusion.1
  370.0 22.5 %cholesky.107 = f32[128,128]{1,0:T(8,128)S(1)} custom-call(f32[128,128]{1,0:T(8,128)S(1)} %convolution_subtract_fusion.1), custom_call_target="Cholesky" | custom-call | tf_op jit(solution)/shard_map/jit(cholesky)/cholesky | solution.py:46
  392.6 0.6 compare_reduce_fusion
  394.5 0.7 fusion.9
  395.2 0.1 triangular_solve.44
  395.3 4.0 while.1
  395.3 0.6 fusion.30
  395.9 1.4 bitcast_dynamic-update-slice_fusion.2
  397.4 0.6 fusion.30
  397.9 1.4 bitcast_dynamic-update-slice_fusion.2
  399.4 19.7 %custom-call.16 = f32[2,128,128]{1,2,0:T(8,128)S(1)} custom-call(f32[2,128,128]{2,1,0:T(8,128)S(1)} %get-tuple-element.9), custom_call_target="InvertDiagBlocksLowerTriangular" | custom-call | tf_op jit(solution)/shard_map/jit(_solve_triangular)/triangular_solve | solution.py:47
  419.0 0.0 all-to-all-done
  419.1 6.8 %fusion.23 = (f32[256,32,256]{2,1,0:T(8,128)S(1)}, f32[256,32,256]{2,1,0:T(8,128)S(1)}) fusion(f32[256,32,512]{2,1,0:T(8,128)} %all-to-all-done), kind=kLoop, calls=%fused_computation.57 | loop fusion | bytes 33554432 | tf_op jit(solution)/shard_map/slice | solution.py:41
  425.8 21.6 %fusion.3 = f32[256,256]{1,0:T(8,128)S(1)} fusion(f32[256,32,256]{2,1,0:T(8,128)S(1)} %get-tuple-element.23, f32[256,32,256]{2,1,0:T(8,128)S(1)} %get-tuple-element.22), kind=kOutput, calls=%fused_computation.9 | convolution fusion | flops 6442450944 | bytes 17039360 | tf_op jit(solution)/shard_map/dot_general | solution.py:40
  447.4 0.3 fusion.10
  447.7 0.3 convolution_subtract_fusion
  448.0 0.3 fusion.13
  448.3 0.7 pad_maximum_fusion
  (13 shorter events, 0.1 us)
Async XLA Ops:
  11.2 6.6 %copy-start = (f32[32,32,256]{2,1,0:T(8,128)S(1)}, f32[32,32,256]{2,1,0:T(8,128)}, u32[]{:S(2)}) copy-start(f32[32,32,256]{2,1,0:T(8,128)} %param.5) | copy-start | bytes 3145732
  34.0 385.1 %all-to-all-start = ((f32[256,32,512]{2,1,0:T(8,128)}), f32[256,32,512]{2,1,0:T(8,128)}, u32[]{:S(2)}, u32[]{:S(2)}) async-start(f32[256,32,512]{2,1,0:T(8,128)} %maximum_select_fusion), calls=%async_computation | async-start | bytes 33554432 | tf_op jit(solution)/shard_map/all_to_all | solution.py:39
  45.7 300.2 %all-reduce.3.cloned.1.call-start = ((), (), s32[]{:S(2)}) async-start(), calls=%async_computation.1 | async-start | bytes 524288 | tf_op jit(solution)/shard_map/psum | solution.py:19
Sparse Core Ops, SparseCore 0:
  51.8 293.9 all-reduce.2
where the time goes:
time: 460 us; the launch traced here: 456 us
  waiting for transfers between devices  297 us (65%)
  other arithmetic  80.6 us (18%)
  matrix products  25.6 us (6%)
  local copies, waits for them, and re-layouts  24.9 us (5%)
  between operations  15.8 us (3%)
  starting transfers between devices  12.1 us (3%)
    psum x1, waiting for transfers between devices, per_device(): diagonal_block = lax.psum(local_diagonal, ('row', 'col'))  297 us
    another operation x6, other arithmetic, per_device(): panel_factor = jnp.linalg.cholesky(diagonal_block)  44.7 us
    dot_general x1, matrix products, per_device(): lax.dot_general(incoming[:, :, :strip_rows], incoming[:, :, strip_rows:],...  21.6 us
    another operation x4, other arithmetic, per_device(): jax.scipy.linalg.solve_triangular(panel_factor, tile_sum, lower=True)  21.1 us
    all_to_all x1, starting transfers between devices, per_device(): lax.all_to_all(outgoing, ('row', 'col'), split_axis=0, concat_axis=0, til...  11.7 us
    select_n x1, other arithmetic, per_device(): jnp.where(filled[:, None, None], jnp.concatenate([send_strip, send_tile],...  11.6 us
  transfers between devices with their start and end apart: 2, of which 1 were waited for; matrix products, arithmetic and copies ran while one was open for 16% of the time, Pallas kernels for 0%

commit v1 on v0

v1 whole, which is shorter than its diff:
```python
import functools

import jax
import jax.numpy as jnp
from jax import lax
from jax.experimental import pallas as pl
from jax.experimental.pallas import tpu as pltpu
from jax.sharding import PartitionSpec as P

AXES = ("row", "col")
MESH = pl.DeviceIdType.MESH
ROWS = ((0, 88), (88, 88), (176, 80))
CUT = 48
STRIDE = (16, 4, 1)
LAG = 6
RING = 8
F32 = jnp.float32


def split(x):
    high = x.astype(jnp.bfloat16)
    return high, (x - high.astype(F32)).astype(jnp.bfloat16)


def dot(a, b):
    return lax.dot_general(a, b, (((1,), (0,)), ((), ())), preferred_element_type=F32)


def kernel(
    item_ref, weight_ref, strip_ref, tile_ref, sum_ref, diagonal_ref,
    strip, tile, left, sent, acc,
    fwd10, fwd11, fwd12, fin10, fin11, fin12,
    fwd20, fwd21, fwd22, fin20, fin21, fin22,
    fwd30, fwd31, fwd32, fin30, fin31, fin32,
    dfull, dpair, dhalf, dx, dquarter, dy, dz, dquarter2, dhalf2,
    load_sem, sib_send, sib_recv,
    fwd1_send, fwd1_recv, fin1_send, fin1_recv,
    fwd2_send, fwd2_recv, fin2_send, fin2_recv,
    fwd3_send, fwd3_recv, fin3_send, fin3_recv,
    d_send, d_recv,
):
    fwd1, fin1 = (fwd10, fwd11, fwd12), (fin10, fin11, fin12)
    fwd2, fin2 = (fwd20, fwd21, fwd22), (fin20, fin21, fin22)
    fwd3, fin3 = (fwd30, fwd31, fwd32), (fin30, fin31, fin32)
    row, col = lax.axis_index("row"), lax.axis_index("col")
    core = lax.rem(row, 2)
    place = (lax.div(row, 2), lax.div(col, 4), lax.rem(col, 4))
    blocks = strip.shape[0]

    def device(y, x, z, c):
        return (y * 2 + c, x * 4 + z)

    def peer(axis, step):
        at = list(place)
        at[axis] = lax.rem(at[axis] + step, 4)
        return device(*at, core)

    sibling = device(*place, 1 - core)

    barrier = pltpu.get_barrier_semaphore()
    partners = [peer(a, s) for a in range(3) for s in (1, 2, 3)] + [sibling]
    for partner in partners:
        pl.semaphore_signal(barrier, inc=1, device_id=partner, device_id_type=MESH)
    get_strip = pltpu.make_async_copy(strip_ref, strip, load_sem.at[0])
    get_tile = pltpu.make_async_copy(tile_ref, tile, load_sem.at[1])
    get_strip.start()
    get_tile.start()
    get_strip.wait()

    left[blocks] = jnp.zeros(left.shape[1:], left.dtype)

    def build(b, carry):
        scaled = strip[b] * weight_ref[b]
        high = scaled.astype(jnp.bfloat16).astype(F32)
        low = scaled - high
        stack = jnp.concatenate([high, high, low, low], axis=0)
        left[b] = stack.T.astype(jnp.bfloat16)
        return carry

    lax.fori_loop(0, blocks, build, 0)
    get_tile.wait()
    pl.semaphore_wait(barrier, len(partners))

    def remote(src, dst, send, recv, to):
        return pltpu.make_async_remote_copy(
            src_ref=src, dst_ref=dst, send_sem=send, recv_sem=recv,
            device_id=to, device_id_type=MESH,
        )

    def product(k, c):
        at = []
        for axis in range(3):
            d = lax.rem(lax.div(k, STRIDE[axis]), 4)
            step = jnp.where(d == 0, 2, jnp.where(d == 1, 1, jnp.where(d == 2, 3, 0)))
            at.append(lax.rem(place[axis] + step, 4))
        number = ((at[0] * 2 + c) * 4 + at[1]) * 4 + at[2]
        lefts, rights = [], []
        for s in range(2):
            slot = item_ref[2 * number + s]
            lefts.append(left[lax.div(slot, 4)])
            high, low = split(tile[lax.rem(slot, tile.shape[0])])
            rights += [high, low, high, low]
        return dot(jnp.concatenate(lefts, axis=1), jnp.concatenate(rights, axis=0))

    def to_sibling(k):
        return remote(
            sent.at[lax.rem(k, RING)], acc.at[k], sib_send.at[k], sib_recv.at[k], sibling
        )

    def send_out(k, carry=0):
        @pl.when(k >= RING)
        def _():
            to_sibling(k - RING).wait_send()

        sent[lax.rem(k, RING)] = product(k, 1 - core)
        to_sibling(k).start()
        return carry

    def rows_of(p):
        return pl.ds(*ROWS[p])

    def fwd_copy(stage, p, way, k, j):
        fwd = (fwd1, fwd2)[stage - 1]
        send, recv = ((fwd1_send, fwd1_recv), (fwd2_send, fwd2_recv))[stage - 1]
        axis = (p + stage - 1) % 3
        return remote(
            acc.at[k, rows_of(p)], fwd[p].at[way, j],
            send.at[p, way, j], recv.at[p, way, j], peer(axis, (1, 3)[way]),
        )

    def fin_copy(stage, p, way, k, j):
        fin = (fin1, fin2)[stage - 1]
        send, recv = ((fin1_send, fin1_recv), (fin2_send, fin2_recv))[stage - 1]
        axis = (p + stage - 1) % 3
        return remote(
            acc.at[k, rows_of(p)], fin[p].at[way, j],
            send.at[p, way, j], recv.at[p, way, j], peer(axis, (1, 3)[way]),
        )

    def take(k, carry=0):
        to_sibling(k).wait_recv()
        acc[k] = acc[k] + product(k, core)
        digit = [lax.rem(lax.div(k, STRIDE[axis]), 4) for axis in range(3)]
        for p in range(3):
            da, db, dc = digit[p], digit[(p + 1) % 3], digit[(p + 2) % 3]
            j, f = db * 2 + lax.rem(dc, 2), db * 4 + dc

            @pl.when((da == 0) & (dc < 2))
            def _():
                fwd_copy(1, p, 0, k, j).start()

            @pl.when((da == 0) & (dc >= 2))
            def _():
                fwd_copy(1, p, 1, k, j).start()

            @pl.when((da == 1) & (dc >= 2))
            def _():
                fin_copy(1, p, 0, k, f).start()

            @pl.when((da == 2) & (dc < 2))
            def _():
                fin_copy(1, p, 1, k, f).start()

        return carry

    def both(k, carry):
        send_out(k + LAG)
        return take(k)

    def diagonal_local(b, carry):
        lefts, rights = [], []
        for s in range(2):
            lefts.append(left[2 * b + s])
            high, low = split(strip[2 * b + s])
            rights += [high, low, high, low]
        dfull[...] = dfull[...] + dot(
            jnp.concatenate(lefts, axis=1), jnp.concatenate(rights, axis=0)
        )
        return carry

    def d_copies(phase):
        py, px, pz = place
        if phase == 0:
            return [remote(dfull.at[pl.ds(128 * (1 - core), 128)], dpair, d_send.at[0, 0], d_recv.at[0, 0], sibling)]
        if phase == 6:
            return [remote(dhalf2, diagonal_ref.at[pl.ds(128 * core, 128)], d_send.at[6, 0], d_recv.at[6, 0], sibling)]
        out = []
        for o in (1, 2, 3):
            if phase == 1:
                src, dst, axis = dhalf.at[pl.ds(32 * lax.rem(px + o, 4), 32)], dx.at[o - 1], 1
            elif phase == 2:
                src, dst, axis = dquarter.at[pl.ds(8 * lax.rem(py + o, 4), 8)], dy.at[o - 1], 0
            elif phase == 3:
                src, dst, axis = dz.at[pz], dz.at[pz], 2
            elif phase == 4:
                part = pl.ds(8 * py, 8)
                src, dst, axis = dquarter2.at[part], dquarter2.at[part], 0
            else:
                part = pl.ds(32 * px, 32)
                src, dst, axis = dhalf2.at[part], dhalf2.at[part], 1
            out.append(remote(src, dst, d_send.at[phase, o - 1], d_recv.at[phase, o - 1], peer(axis, o)))
        return out

    def d_arrive(phase):
        py, px, pz = place
        for o, copy in enumerate(d_copies(phase)):
            copy.wait_recv()
        if phase == 0:
            dhalf[...] = dfull[pl.ds(128 * core, 128)] + dpair[...]
        elif phase == 1:
            dquarter[...] = dhalf[pl.ds(32 * px, 32)] + dx[0] + dx[1] + dx[2]
        elif phase == 2:
            dz[pz] = dquarter[pl.ds(8 * py, 8)] + dy[0] + dy[1] + dy[2]
        elif phase == 3:
            dquarter2[pl.ds(8 * py, 8)] = dz[0] + dz[1] + dz[2] + dz[3]
        elif phase == 4:
            dhalf2[pl.ds(32 * px, 32)] = dquarter2[...]
        elif phase == 5:
            diagonal_ref[pl.ds(128 * core, 128)] = dhalf2[...]

    def d_start(phase):
        for copy in d_copies(phase):
            copy.start()

    lax.fori_loop(0, LAG, send_out, 0)
    lax.fori_loop(0, 16, both, 0)
    dfull[...] = jnp.zeros_like(dfull)
    lax.fori_loop(0, blocks // 2, diagonal_local, 0)
    d_start(0)
    at = 16
    for phase in range(6):
        lax.fori_loop(at, at + 7, both, 0)
        at += 7
        d_arrive(phase)
        d_start(phase + 1)
    lax.fori_loop(at, 64, lambda k, c: take(k), 0)
    d_arrive(6)

    def slot(p, da, db, dc):
        digit = [0, 0, 0]
        digit[p], digit[(p + 1) % 3], digit[(p + 2) % 3] = da, db, dc
        return digit[0] * 16 + digit[1] * 4 + digit[2]

    for j in range(8):
        db = j // 2
        for p in range(3):
            for way in range(2):
                dc = j % 2 + 2 * way
                k = slot(p, 1 + way, db, dc)
                fwd_copy(1, p, way, k, j).wait_recv()
                acc[k, rows_of(p)] = acc[k, rows_of(p)] + fwd1[p][way, j]
                fin_copy(1, p, way, k, db * 4 + dc).start()
    for f in range(16):
        db, dc = f // 4, f % 4
        for p in range(3):
            k = slot(p, 3, db, dc)
            for way in range(2):
                fin_copy(1, p, way, k, f).wait_recv()
            acc[k, rows_of(p)] = acc[k, rows_of(p)] + fin1[p][0, f] + fin1[p][1, f]
            if db == 0:
                fwd_copy(2, p, dc // 2, k, dc % 2).start()
            if db == 1 and dc >= 2:
                fin_copy(2, p, 0, k, dc).start()
            if db == 2 and dc < 2:
                fin_copy(2, p, 1, k, dc).start()
    for j in range(2):
        for p in range(3):
            for way in range(2):
                dc = j + 2 * way
                k = slot(p, 3, 1 + way, dc)
                fwd_copy(2, p, way, k, j).wait_recv()
                acc[k, rows_of(p)] = acc[k, rows_of(p)] + fwd2[p][way, j]
                fin_copy(2, p, way, k, dc).start()

    def part3(p, way):
        low, size = ROWS[p]
        return (low, CUT) if way == 0 else (low + CUT, size - CUT)

    def fwd3_copy(p, way):
        low, size = part3(p, way)
        return remote(
            acc.at[slot(p, 3, 3, 0), pl.ds(low, size)], fwd3[p].at[way, pl.ds(0, size)],
            fwd3_send.at[p, way], fwd3_recv.at[p, way], peer((p + 2) % 3, (1, 3)[way]),
        )

    def fin3_copy(p, way, half):
        low, size = part3(p, half)
        return remote(
            acc.at[slot(p, 3, 3, 1 + way), pl.ds(low, size)],
            fin3[p].at[way, pl.ds(low - ROWS[p][0], size)],
            fin3_send.at[p, way, half], fin3_recv.at[p, way, half],
            peer((p + 2) % 3, (1, 3)[way]),
        )

    for dc in range(4):
        for p in range(3):
            k = slot(p, 3, 3, dc)
            for way in range(2):
                fin_copy(2, p, way, k, dc).wait_recv()
            acc[k, rows_of(p)] = acc[k, rows_of(p)] + fin2[p][0, dc] + fin2[p][1, dc]
            if dc == 0:
                fwd3_copy(p, 0).start()
                fwd3_copy(p, 1).start()
            if dc == 1:
                fin3_copy(p, 0, 1).start()
            if dc == 2:
                fin3_copy(p, 1, 0).start()
    for p in range(3):
        for way in range(2):
            low, size = part3(p, way)
            k = slot(p, 3, 3, 1 + way)
            fwd3_copy(p, way).wait_recv()
            acc[k, pl.ds(low, size)] = acc[k, pl.ds(low, size)] + fwd3[p][way, pl.ds(0, size)]
            fin3_copy(p, way, way).start()
    for p in range(3):
        for way in range(2):
            for half in range(2):
                fin3_copy(p, way, half).wait_recv()
        sum_ref[rows_of(p)] = acc[63, rows_of(p)] + fin3[p][0] + fin3[p][1]

    def drain_ring(k, carry):
        to_sibling(k).wait_send()
        return carry

    lax.fori_loop(64 - RING, 64, drain_ring, 0)
    for phase in range(7):
        for copy in d_copies(phase):
            copy.wait_send()

    def drain(i, carry):
        for p in range(3):
            for way in range(2):
                fin_copy(1, p, way, 0, i).wait_send()
        return carry

    def drain_half(i, carry):
        for p in range(3):
            for way in range(2):
                fwd_copy(1, p, way, 0, i).wait_send()
        return carry

    lax.fori_loop(0, 16, drain, 0)
    lax.fori_loop(0, 8, drain_half, 0)
    for p in range(3):
        for way in range(2):
            for j in range(2):
                fwd_copy(2, p, way, 0, j).wait_send()
                fin3_copy(p, way, j).wait_send()
            for j in range(4):
                fin_copy(2, p, way, 0, j).wait_send()
            fwd3_copy(p, way).wait_send()


def gather_and_sum(item, weight, strip_columns, tiles):
    blocks, width, rows = strip_columns.shape
    items = tiles.shape[0]
    dma = pltpu.SemaphoreType.DMA
    vmem = lambda *shape: pltpu.VMEM(shape, F32)
    sizes = [size for _, size in ROWS]
    any_space = pl.BlockSpec(memory_space=pl.ANY)
    in_vmem = pl.BlockSpec(memory_space=pltpu.VMEM)
    return pl.pallas_call(
        kernel,
        out_shape=[jax.ShapeDtypeStruct((256, 256), F32)] * 2,
        in_specs=[pl.BlockSpec(memory_space=pltpu.SMEM), in_vmem, any_space, any_space],
        out_specs=[in_vmem, in_vmem],
        scratch_shapes=[
            vmem(blocks, width, rows), vmem(items, width, rows),
            pltpu.VMEM((blocks + 1, rows, 4 * width), jnp.bfloat16),
            vmem(RING, 256, 256), vmem(64, 256, 256),
            *[vmem(2, 8, s, 256) for s in sizes], *[vmem(2, 16, s, 256) for s in sizes],
            *[vmem(2, 2, s, 256) for s in sizes], *[vmem(2, 4, s, 256) for s in sizes],
            *[vmem(2, CUT, 256) for s in sizes], *[vmem(2, s, 256) for s in sizes],
            vmem(256, 256), vmem(128, 256), vmem(128, 256), vmem(3, 32, 256), vmem(32, 256),
            vmem(3, 8, 256), vmem(4, 8, 256), vmem(32, 256), vmem(128, 256),
            dma((2,)), dma((64,)), dma((64,)),
            dma((3, 2, 8)), dma((3, 2, 8)), dma((3, 2, 16)), dma((3, 2, 16)),
            dma((3, 2, 2)), dma((3, 2, 2)), dma((3, 2, 4)), dma((3, 2, 4)),
            dma((3, 2)), dma((3, 2)), dma((3, 2, 2)), dma((3, 2, 2)),
            dma((7, 3)), dma((7, 3)),
        ],
        compiler_params=pltpu.CompilerParams(
            collective_id=0, has_side_effects=True, vmem_limit_bytes=60 << 20
        ),
    )(item, weight, strip_columns, tiles)


def per_device(strip_columns, tile_columns, barrier_weights, column_counts, tile_lists):
    highest = lax.Precision.HIGHEST
    blocks, width, rows = strip_columns.shape
    touched = tile_columns.shape[1]
    own_width = tile_columns.shape[3]
    devices = lax.axis_size(AXES)
    items = blocks * touched
    live_mask = jnp.arange(width, dtype=jnp.int32)[None, :] < column_counts[:, None]
    live_weight = jnp.where(live_mask, barrier_weights, 0.0)
    listed = tile_lists.reshape(1, items) == jnp.arange(devices, dtype=jnp.int32)[:, None]
    number = jnp.arange(items, dtype=jnp.int32)[None, :]
    least = jnp.min(jnp.where(listed, number, items), axis=1)
    most = jnp.max(jnp.where(listed, number, -1), axis=1)
    most = jnp.where((most == least) | (most < 0), items, most)
    slot = jnp.stack([least, most], axis=1).reshape(devices * 2)
    tile_sum, diagonal = gather_and_sum(
        slot,
        live_weight[:, :, None],
        strip_columns,
        tile_columns.reshape(items, width, own_width),
    )
    factor = jnp.linalg.cholesky(diagonal)
    inverse = jax.scipy.linalg.solve_triangular(
        factor, jnp.eye(rows, dtype=factor.dtype), lower=True
    )
    return (factor, jnp.dot(inverse, tile_sum, precision=highest))


def solution(mesh):
    return jax.shard_map(
        per_device,
        mesh=mesh,
        in_specs=(
            P(AXES, None, None),
            P(AXES, None, None, None),
            P(AXES, None),
            P(AXES),
            P(AXES, None),
        ),
        out_specs=(P(), P(None, AXES)),
        check_vma=False,
    )
```

time: 460 us -> 175 us (0.38)
  waiting for transfers between devices: 297 us -> 0 us
  Pallas kernels: 0 us -> 106 us
  other arithmetic: 80.6 us -> 56.5 us
  matrix products: 25.6 us -> 2.4 us
  local copies, waits for them, and re-layouts: 24.9 us -> 7.99 us
  between operations: 15.8 us -> 2.07 us
  starting transfers between devices: 12.1 us -> 0 us
    psum x1 -> x0, waiting for transfers between devices: 297 us -> none  [per_device(): diagonal_block = lax.psum(local_diagonal, ('row', 'col'))]
    pallas_call x0 -> x1, Pallas kernels: none -> 106 us  [gather_and_sum(): pl.pallas_call(kernel, out_shape=[jax.ShapeDtypeStruct((256, 256), F32)]...]
    dot_general x2 -> x1, matrix products: 24.3 us -> 1.09 us  [per_device(): return (factor, jnp.dot(inverse, tile_sum, precision=highest))]
    select_n x4 -> x1, other arithmetic: 12.5 us -> 0.01 us  [per_device(): most = jnp.where((most == least) | (most < 0), items, most)]
    all_to_all x1 -> x0, starting transfers between devices: 11.7 us -> none  [per_device(): lax.all_to_all(outgoing, ('row', 'col'), split_axis=0, concat_axis=0, til...]
    another operation x11 -> x10, other arithmetic: 66.1 us -> 54.6 us  [the longest x6 33.9 us: per_device(): factor = jnp.linalg.cholesky(diagonal)]
    gather x2 -> x0, local copies, waits for them, and re-layouts: 10.9 us -> none  [the longest x1 6.59 us: per_device(): send_tile = tile_columns.reshape(item_count, block_width, own_width)[picked]]
    slice x1 -> x0, local copies, waits for them, and re-layouts: 6.76 us -> none  [per_device(): incoming[:, :, :strip_rows]]
  transfers between devices with their start and end apart: 2 -> 0, of which waited for: 1 -> 0; matrix products, arithmetic and copies ran while one was open for 16% -> 0% of each run, Pallas kernels for 0% -> 0%
where the time goes in v1:
time: 175 us
  Pallas kernels  106 us (61%)
  other arithmetic  56.5 us (32%)
  local copies, waits for them, and re-layouts  7.99 us (5%)
  matrix products  2.4 us (1%)
  between operations  2.07 us (1%)
    pallas_call x1, Pallas kernels, gather_and_sum(): pl.pallas_call(kernel, out_shape=[jax.ShapeDtypeStruct((256, 256), F32)]...  106 us
    another operation x6, other arithmetic, per_device(): factor = jnp.linalg.cholesky(diagonal)  33.9 us
    another operation x3, other arithmetic, per_device(): jax.scipy.linalg.solve_triangular(factor, jnp.eye(rows, dtype=factor.dtyp...  20.6 us
    another operation x6, local copies, waits for them, and re-layouts  4.02 us

profile of v1, /device:TPU:0, one launch (start us, length us, event | category | flops | bytes accessed | tf_op | source)
XLA Modules:
  0.0 174.8 jit_solution(14547907805882306494)
XLA Ops:
  0.6 0.8 copy.13
  1.4 0.1 eq.30
  1.5 0.1 select_reduce_fusion.3
  1.6 0.1 copy.14
  1.8 0.7 reshape.52.item_ref
  2.5 0.8 select_bitcast_fusion.1
  3.3 1.1 copy.15.weight_ref
  4.3 105.8 %shard_map.68 = (f32[256,256]{1,0:T(8,128)}, f32[256,256]{1,0:T(8,128)}) custom-call(s32[256]{0:T(256)} %reshape.52.item_ref, f32[32,32,1]{2,1,0:T(8,128)} %copy.15.weight_ref, f32[32,32,256]{2,1,0:T(8,128)} %strip_ref.1, f32[128,32,256]{2,1,0:T(8,128)} %bitcast.39), custom_call_target="tpu_custom_call" | custom-call | tf_op jit(solution)/shard_map/pallas_call | solution.py:362
  110.2 0.0 copy-start
  110.2 1.1 copy.16
  111.3 1.0 fusion.4
  112.3 11.7 %cholesky.52 = f32[128,128]{1,0:T(8,128)S(1)} custom-call(f32[128,128]{1,0:T(8,128)S(1)} %cholesky.121), custom_call_target="Cholesky" | custom-call | tf_op jit(solution)/shard_map/jit(cholesky)/cholesky | solution.py:409
  124.1 9.8 %custom-call.15 = f32[1,128,128]{1,2,0:T(8,128)S(1)} custom-call(f32[1,128,128]{2,1,0:T(8,128)S(1)} %get-tuple-element.31), custom_call_target="InvertDiagBlocksLowerTriangular" | custom-call | tf_op jit(solution)/shard_map/jit(cholesky)/cholesky | solution.py:409
  133.9 0.2 constant_dynamic-update-slice_fusion.1
  134.1 0.3 convolution_subtract_fusion.1
  134.4 11.7 %cholesky.108 = f32[128,128]{1,0:T(8,128)S(1)} custom-call(f32[128,128]{1,0:T(8,128)S(1)} %convolution_subtract_fusion.1), custom_call_target="Cholesky" | custom-call | tf_op jit(solution)/shard_map/jit(cholesky)/cholesky | solution.py:409
  146.1 0.6 compare_reduce_fusion
  148.1 0.7 fusion.5
  148.8 0.1 triangular_solve.44
  148.9 4.1 %while.1 = (s32[]{:T(128)}, f32[256,256]{1,0:T(8,128)S(1)}, s32[2,2]{1,0:T(2,128)S(1)}, f32[2,128,128]{2,1,0:T(8,128)S(1)}, s32[]{:T(128)}) while((s32[]{:T(128)}, f32[256,256]{1,0:T(8,128)S(1)}, s32[2,2]{1,0:T(2,128)S(1)}, f32[2,128,128]{2,1,0:T(8,128)S(1)}, s32[]{:T(128)}) %tuple.29), condition=%wide.while_cond, body=%wide.while_body.sunk | while | flops 2 | bytes 131189 | solution.py:410
  148.9 0.7 fusion.21
  149.6 1.3 bitcast_dynamic-update-slice_fusion.2
  151.0 0.7 fusion.21
  151.6 1.3 bitcast_dynamic-update-slice_fusion.2
  153.0 19.9 %custom-call.16 = f32[2,128,128]{1,2,0:T(8,128)S(1)} custom-call(f32[2,128,128]{2,1,0:T(8,128)S(1)} %get-tuple-element.13), custom_call_target="InvertDiagBlocksLowerTriangular" | custom-call | tf_op jit(solution)/shard_map/jit(_solve_triangular)/triangular_solve | solution.py:410
  172.9 0.3 fusion.6
  173.2 0.3 convolution_subtract_fusion
  173.4 0.3 fusion.9
  173.7 0.0 copy-done
  173.8 1.1 fusion
  (11 shorter events, 0.2 us)
Async XLA Ops:
  110.2 63.6 %copy-start = (f32[256,256]{1,0:T(8,128)S(1)}, f32[256,256]{1,0:T(8,128)}, u32[]{:S(2)}) copy-start(f32[256,256]{1,0:T(8,128)} %get-tuple-element.5) | copy-start | bytes 786436

commit v2 on v1

--- a/solution.py
+++ b/solution.py
@@ -11,9 +11,12 @@
 MESH = pl.DeviceIdType.MESH
 ROWS = ((0, 88), (88, 88), (176, 80))
 CUT = 48
+PACE = 5
+SECOND = (88, 92, 100, 106, 112, 118, 126)
 STRIDE = (16, 4, 1)
-LAG = 6
-RING = 8
+LAG = 2
+RING = 16
+OFFSET = (2, 1, 3, 0)
 F32 = jnp.float32
 
 
@@ -26,13 +29,80 @@
     return lax.dot_general(a, b, (((1,), (0,)), ((), ())), preferred_element_type=F32)
 
 
+def full_dot(a, b, turned=False):
+    return lax.dot_general(
+        a, b, (((1,), (1 if turned else 0,)), ((), ())),
+        precision=lax.Precision.HIGHEST, preferred_element_type=F32,
+    )
+
+
+def diagonal_of(r):
+    i = lax.broadcasted_iota(jnp.int32, (r, r), 0)
+    return i, lax.broadcasted_iota(jnp.int32, (r, r), 1)
+
+
+def open_block(a):
+    i, j = diagonal_of(128)
+    both = jnp.concatenate([a, jnp.where(i == j, 1.0, 0.0)], axis=1)
+    return [both[8 * g : 8 * g + 8] for g in range(16)]
+
+
+def eliminate(groups):
+    below = lax.broadcasted_iota(jnp.int32, (8, 1), 0)
+    for k in range(0, 128, 2):
+        top, s = k // 8, k % 8
+        one, two = groups[top][s : s + 1], groups[top][s + 1 : s + 2]
+        a, b, c = one[:, k : k + 1], one[:, k + 1 : k + 2], two[:, k + 1 : k + 2]
+        first = 1.0 / a
+        second = a / (a * c - b * b)
+        ratio = b * first
+        scaled_one, scaled_two = one * first, (two - ratio * one) * second
+        for g in range(top, 16):
+            left = groups[g][:, k : k + 1]
+            right = groups[g][:, k + 1 : k + 2] - ratio * left
+            if g == top:
+                left = jnp.where(below > s, left, 0.0)
+                right = jnp.where(below > s + 1, right, 0.0)
+            groups[g] = groups[g] - left * scaled_one - right * scaled_two
+        yield
+
+
+def close_block(groups):
+    both = jnp.concatenate(groups, axis=0)
+    i, j = diagonal_of(128)
+    pivots = jnp.sum(jnp.where(i == j, both[:, :128], 0.0), axis=1, keepdims=True)
+    both = both * (1.0 / jnp.sqrt(pivots))
+    return jnp.where(j >= i, both[:, :128], 0.0).T, both[:, 128:]
+
+
+def factorize(d_ref, l_ref, inverse_ref):
+    groups = open_block(d_ref[:128, :128])
+    yield from eliminate(groups)
+    upper, upper_inverse = close_block(groups)
+    between = full_dot(d_ref[128:, :128], upper_inverse, True)
+    zero = jnp.zeros((128, 128), F32)
+    l_ref[:128, :128] = upper
+    l_ref[:128, 128:] = zero
+    l_ref[128:, :128] = between
+    inverse_ref[:128, :128] = upper_inverse
+    inverse_ref[:128, 128:] = zero
+    groups = open_block(d_ref[128:, 128:] - full_dot(between, between, True))
+    yield from eliminate(groups)
+    lower, lower_inverse = close_block(groups)
+    l_ref[128:, 128:] = lower
+    inverse_ref[128:, 128:] = lower_inverse
+    inverse_ref[128:, :128] = -full_dot(
+        lower_inverse, full_dot(l_ref[128:, :128], inverse_ref[:128, :128])
+    )
+
+
 def kernel(
-    item_ref, weight_ref, strip_ref, tile_ref, sum_ref, diagonal_ref,
+    item_ref, weight_ref, strip_ref, tile_ref, factor_ref, update_ref,
     strip, tile, left, sent, acc,
     fwd10, fwd11, fwd12, fin10, fin11, fin12,
     fwd20, fwd21, fwd22, fin20, fin21, fin22,
     fwd30, fwd31, fwd32, fin30, fin31, fin32,
-    dfull, dpair, dhalf, dx, dquarter, dy, dz, dquarter2, dhalf2,
+    inverse_ref, total, diagonal_ref, dfull, dpair, dhalf, dx, dquarter, dy, dz, dquarter2, dhalf2,
     load_sem, sib_send, sib_recv,
     fwd1_send, fwd1_recv, fin1_send, fin1_recv,
     fwd2_send, fwd2_recv, fin2_send, fin2_recv,
@@ -87,34 +157,28 @@
             device_id=to, device_id_type=MESH,
         )
 
-    def product(k, c):
-        at = []
-        for axis in range(3):
-            d = lax.rem(lax.div(k, STRIDE[axis]), 4)
-            step = jnp.where(d == 0, 2, jnp.where(d == 1, 1, jnp.where(d == 2, 3, 0)))
-            at.append(lax.rem(place[axis] + step, 4))
-        number = ((at[0] * 2 + c) * 4 + at[1]) * 4 + at[2]
+    def product(ty, tx, tz, c):
+        number = ((ty * 2 + c) * 4 + tx) * 4 + tz
         lefts, rights = [], []
-        for s in range(2):
-            slot = item_ref[2 * number + s]
+        for n in range(2):
+            slot = item_ref[2 * number + n]
             lefts.append(left[lax.div(slot, 4)])
             high, low = split(tile[lax.rem(slot, tile.shape[0])])
             rights += [high, low, high, low]
         return dot(jnp.concatenate(lefts, axis=1), jnp.concatenate(rights, axis=0))
 
+    def offset(d):
+        return jnp.where(d == 0, 2, jnp.where(d == 1, 1, jnp.where(d == 2, 3, 0)))
+
+    def group_tiles(i, c):
+        ty = lax.rem(place[0] + offset(lax.div(i, 4)), 4)
+        tx = lax.rem(place[1] + offset(lax.rem(i, 4)), 4)
+        return [functools.partial(product, ty, tx, lax.rem(place[2] + o, 4), c) for o in OFFSET]
+
     def to_sibling(k):
         return remote(
             sent.at[lax.rem(k, RING)], acc.at[k], sib_send.at[k], sib_recv.at[k], sibling
         )
-
-    def send_out(k, carry=0):
-        @pl.when(k >= RING)
-        def _():
-            to_sibling(k - RING).wait_send()
-
-        sent[lax.rem(k, RING)] = product(k, 1 - core)
-        to_sibling(k).start()
-        return carry
 
     def rows_of(p):
         return pl.ds(*ROWS[p])
@@ -125,7 +189,7 @@
         axis = (p + stage - 1) % 3
         return remote(
             acc.at[k, rows_of(p)], fwd[p].at[way, j],
-            send.at[p, way, j], recv.at[p, way, j], peer(axis, (1, 3)[way]),
+            send.at[p, way, j], recv.at[p, way, j], peer(axis, 1 + 2 * way),
         )
 
     def fin_copy(stage, p, way, k, j):
@@ -134,38 +198,78 @@
         axis = (p + stage - 1) % 3
         return remote(
             acc.at[k, rows_of(p)], fin[p].at[way, j],
-            send.at[p, way, j], recv.at[p, way, j], peer(axis, (1, 3)[way]),
-        )
-
-    def take(k, carry=0):
-        to_sibling(k).wait_recv()
-        acc[k] = acc[k] + product(k, core)
-        digit = [lax.rem(lax.div(k, STRIDE[axis]), 4) for axis in range(3)]
+            send.at[p, way, j], recv.at[p, way, j], peer(axis, 1 + 2 * way),
+        )
+
+    def send_on(i, dz):
+        k = 4 * i + dz
+        digit = (lax.div(i, 4), lax.rem(i, 4), dz)
         for p in range(3):
             da, db, dc = digit[p], digit[(p + 1) % 3], digit[(p + 2) % 3]
-            j, f = db * 2 + lax.rem(dc, 2), db * 4 + dc
-
-            @pl.when((da == 0) & (dc < 2))
+            if p == 2 and dz == 3:
+                continue
+
+            if p != 2 or dz == 0:
+                @pl.when(da == 0)
+                def _():
+                    way = jnp.where(dc < 2, 0, 1)
+                    fwd_copy(1, p, way, k, db * 2 + lax.rem(dc, 2)).start()
+
+            if p != 2 or dz > 0:
+                @pl.when(((da == 1) & (dc >= 2)) | ((da == 2) & (dc < 2)))
+                def _():
+                    fin_copy(1, p, da - 1, k, db * 4 + dc).start()
+
+    def give_group(i, fresh=False):
+        for n, term in enumerate(group_tiles(i, 1 - core)):
+            sent[lax.rem(4 * i + n, RING)] = term()
+
+    def give(i, carry):
+        give_group(i)
+        for n in range(4):
+            to_sibling(4 * i + n).start()
+        return carry
+
+    def take_group(i):
+        for n, term in enumerate(group_tiles(i, core)):
+            acc[4 * i + n] = acc[4 * i + n] + term()
+
+    def take(i, carry):
+        for n in range(4):
+            to_sibling(4 * i + n).wait_recv()
+        take_group(i)
+        for n in range(4):
+            send_on(i, n)
+        return carry
+
+    def both(i, carry):
+        @pl.when(i >= RING // 4 - LAG)
+        def _():
+            for n in range(4):
+                to_sibling(4 * (i + LAG) - RING + n).wait_send()
+
+        for n in range(4):
+            to_sibling(4 * i + n).wait_recv()
+        give_group(i + LAG)
+        take_group(i)
+        for n in range(4):
+            to_sibling(4 * (i + LAG) + n).start()
+        for n in range(4):
+            send_on(i, n)
+
+        @pl.when(i == 3)
+        def _():
+            dfull[...] = jnp.zeros_like(dfull)
+            lax.fori_loop(0, blocks // 2, diagonal_local, 0)
+            d_start(0)
+
+        for phase, after in enumerate((5, 7, 9, 11, 13)):
+            @pl.when(i == after)
             def _():
-                fwd_copy(1, p, 0, k, j).start()
-
-            @pl.when((da == 0) & (dc >= 2))
-            def _():
-                fwd_copy(1, p, 1, k, j).start()
-
-            @pl.when((da == 1) & (dc >= 2))
-            def _():
-                fin_copy(1, p, 0, k, f).start()
-
-            @pl.when((da == 2) & (dc < 2))
-            def _():
-                fin_copy(1, p, 1, k, f).start()
-
-        return carry
-
-    def both(k, carry):
-        send_out(k + LAG)
-        return take(k)
+                d_arrive(phase)
+                d_start(phase + 1)
+
+        return carry
 
     def diagonal_local(b, carry):
         lefts, rights = [], []
@@ -222,19 +326,11 @@
         for copy in d_copies(phase):
             copy.start()
 
-    lax.fori_loop(0, LAG, send_out, 0)
-    lax.fori_loop(0, 16, both, 0)
-    dfull[...] = jnp.zeros_like(dfull)
-    lax.fori_loop(0, blocks // 2, diagonal_local, 0)
-    d_start(0)
-    at = 16
-    for phase in range(6):
-        lax.fori_loop(at, at + 7, both, 0)
-        at += 7
-        d_arrive(phase)
-        d_start(phase + 1)
-    lax.fori_loop(at, 64, lambda k, c: take(k), 0)
-    d_arrive(6)
+    lax.fori_loop(0, LAG, give, 0)
+    lax.fori_loop(0, 16 - LAG, both, 0)
+    lax.fori_loop(16 - LAG, 16, take, 0)
+    d_arrive(5)
+    d_start(6)
 
     def slot(p, da, db, dc):
         digit = [0, 0, 0]
@@ -250,7 +346,7 @@
                 fwd_copy(1, p, way, k, j).wait_recv()
                 acc[k, rows_of(p)] = acc[k, rows_of(p)] + fwd1[p][way, j]
                 fin_copy(1, p, way, k, db * 4 + dc).start()
-    for f in range(16):
+    def gather1(f):
         db, dc = f // 4, f % 4
         for p in range(3):
             k = slot(p, 3, db, dc)
@@ -263,7 +359,7 @@
                 fin_copy(2, p, 0, k, dc).start()
             if db == 2 and dc < 2:
                 fin_copy(2, p, 1, k, dc).start()
-    for j in range(2):
+    def pass2(j):
         for p in range(3):
             for way in range(2):
                 dc = j + 2 * way
@@ -292,7 +388,7 @@
             peer((p + 2) % 3, (1, 3)[way]),
         )
 
-    for dc in range(4):
+    def gather2(dc):
         for p in range(3):
             k = slot(p, 3, 3, dc)
             for way in range(2):
@@ -305,18 +401,36 @@
                 fin3_copy(p, 0, 1).start()
             if dc == 2:
                 fin3_copy(p, 1, 0).start()
-    for p in range(3):
-        for way in range(2):
-            low, size = part3(p, way)
-            k = slot(p, 3, 3, 1 + way)
-            fwd3_copy(p, way).wait_recv()
-            acc[k, pl.ds(low, size)] = acc[k, pl.ds(low, size)] + fwd3[p][way, pl.ds(0, size)]
-            fin3_copy(p, way, way).start()
-    for p in range(3):
-        for way in range(2):
-            for half in range(2):
-                fin3_copy(p, way, half).wait_recv()
-        sum_ref[rows_of(p)] = acc[63, rows_of(p)] + fin3[p][0] + fin3[p][1]
+    def pass3():
+        for p in range(3):
+            for way in range(2):
+                low, size = part3(p, way)
+                k = slot(p, 3, 3, 1 + way)
+                fwd3_copy(p, way).wait_recv()
+                acc[k, pl.ds(low, size)] = acc[k, pl.ds(low, size)] + fwd3[p][way, pl.ds(0, size)]
+                fin3_copy(p, way, way).start()
+
+    def gather3():
+        for p in range(3):
+            for way in range(2):
+                for half in range(2):
+                    fin3_copy(p, way, half).wait_recv()
+            total[rows_of(p)] = acc[63, rows_of(p)] + fin3[p][0] + fin3[p][1]
+
+    d_arrive(6)
+    moves = {PACE * (f + 1): functools.partial(gather1, f) for f in range(16)}
+    moves |= {SECOND[j]: functools.partial(pass2, j) for j in range(2)}
+    moves |= {SECOND[2 + dc]: functools.partial(gather2, dc) for dc in range(4)}
+    moves[SECOND[6]] = pass3
+    step = 0
+    for _ in factorize(diagonal_ref, factor_ref, inverse_ref):
+        step += 1
+        if step in moves:
+            moves.pop(step)()
+    for step in sorted(moves):
+        moves[step]()
+    gather3()
+    update_ref[...] = full_dot(inverse_ref[...], total[...])
 
     def drain_ring(k, carry):
         to_sibling(k).wait_send()
@@ -371,6 +485,7 @@
             *[vmem(2, 8, s, 256) for s in sizes], *[vmem(2, 16, s, 256) for s in sizes],
             *[vmem(2, 2, s, 256) for s in sizes], *[vmem(2, 4, s, 256) for s in sizes],
             *[vmem(2, CUT, 256) for s in sizes], *[vmem(2, s, 256) for s in sizes],
+            vmem(256, 256), vmem(256, 256), vmem(256, 256),
             vmem(256, 256), vmem(128, 256), vmem(128, 256), vmem(3, 32, 256), vmem(32, 256),
             vmem(3, 8, 256), vmem(4, 8, 256), vmem(32, 256), vmem(128, 256),
             dma((2,)), dma((64,)), dma((64,)),
@@ -386,7 +501,6 @@
 
 
 def per_device(strip_columns, tile_columns, barrier_weights, column_counts, tile_lists):
-    highest = lax.Precision.HIGHEST
     blocks, width, rows = strip_columns.shape
     touched = tile_columns.shape[1]
     own_width = tile_columns.shape[3]
@@ -400,17 +514,12 @@
     most = jnp.max(jnp.where(listed, number, -1), axis=1)
     most = jnp.where((most == least) | (most < 0), items, most)
     slot = jnp.stack([least, most], axis=1).reshape(devices * 2)
-    tile_sum, diagonal = gather_and_sum(
+    return gather_and_sum(
         slot,
         live_weight[:, :, None],
         strip_columns,
         tile_columns.reshape(items, width, own_width),
     )
-    factor = jnp.linalg.cholesky(diagonal)
-    inverse = jax.scipy.linalg.solve_triangular(
-        factor, jnp.eye(rows, dtype=factor.dtype), lower=True
-    )
-    return (factor, jnp.dot(inverse, tile_sum, precision=highest))
 
 
 def solution(mesh):

time: 175 us -> 118 us (0.67)
  other arithmetic: 56.5 us -> 0.92 us
  Pallas kernels: 106 us -> 109 us
  matrix products: 2.4 us -> 0 us
  local copies, waits for them, and re-layouts: 7.99 us -> 6.08 us
    another operation x9 -> x0, other arithmetic: 54.6 us -> none  [the longest x6 33.9 us: per_device(): factor = jnp.linalg.cholesky(diagonal)]
    another operation x9 -> x0, local copies, waits for them, and re-layouts: 4.12 us -> none
    unnamed x3, local copies, waits for them, and re-layouts: 0.77 us -> 4.1 us
    pallas_call x1, Pallas kernels: 106 us -> 109 us  [gather_and_sum(): pl.pallas_call(kernel, out_shape=[jax.ShapeDtypeStruct((256, 256), F32)]...]
where the time goes in v2:
time: 118 us; the launch traced here: 116 us
  Pallas kernels  109 us (92%)
  local copies, waits for them, and re-layouts  6.08 us (5%)
    pallas_call x1, Pallas kernels, gather_and_sum(): pl.pallas_call(kernel, out_shape=[jax.ShapeDtypeStruct((256, 256), F32)]...  109 us
    unnamed x3, local copies, waits for them, and re-layouts  4.1 us

profile of v2, /device:TPU:0, one launch (start us, length us, event | category | flops | bytes accessed | tf_op | source)
XLA Modules:
  0.0 116.5 jit_solution(14706384127453818341)
XLA Ops:
  0.6 0.8 select_bitcast_fusion
  1.4 0.8 copy.11
  2.2 0.1 eq.25
  2.3 0.1 select_reduce_fusion.1
  2.4 0.1 copy.12
  2.6 0.7 reshape.33.item_ref
  3.3 1.1 copy.13.weight_ref
  4.3 108.8 %shard_map.68 = (f32[256,256]{1,0:T(8,128)}, f32[256,256]{1,0:T(8,128)}) custom-call(s32[256]{0:T(256)} %reshape.33.item_ref, f32[32,32,1]{2,1,0:T(8,128)} %copy.13.weight_ref, f32[32,32,256]{2,1,0:T(8,128)} %strip_ref.1, f32[128,32,256]{2,1,0:T(8,128)} %bitcast.7), custom_call_target="tpu_custom_call" | custom-call | tf_op jit(solution)/shard_map/pallas_call | solution.py:476
  113.1 1.7 %copy.16 = f32[256,256]{1,0:T(8,128)} copy(f32[256,256]{1,0:T(8,128)} %get-tuple-element.6) | data formatting | bytes 524288
  114.8 1.7 %copy.17 = f32[256,256]{1,0:T(8,128)} copy(f32[256,256]{1,0:T(8,128)} %get-tuple-element.7) | data formatting | bytes 524288
  (2 shorter events, 0.0 us)

commit v3 on v2

--- a/solution.py
+++ b/solution.py
@@ -11,12 +11,10 @@
 MESH = pl.DeviceIdType.MESH
 ROWS = ((0, 88), (88, 88), (176, 80))
 CUT = 48
+TURNS = (1, 4, 8)
 PACE = 5
 SECOND = (88, 92, 100, 106, 112, 118, 126)
 STRIDE = (16, 4, 1)
-LAG = 2
-RING = 16
-OFFSET = (2, 1, 3, 0)
 F32 = jnp.float32
 
 
@@ -97,12 +95,12 @@
 
 
 def kernel(
-    item_ref, weight_ref, strip_ref, tile_ref, factor_ref, update_ref,
-    strip, tile, left, sent, acc,
+    weight_ref, count_ref, list_ref, strip_ref, tile_ref, factor_ref, update_ref,
+    strip, scaled, tile, left, lives, slots, table, acc,
     fwd10, fwd11, fwd12, fin10, fin11, fin12,
     fwd20, fwd21, fwd22, fin20, fin21, fin22,
     fwd30, fwd31, fwd32, fin30, fin31, fin32,
-    inverse_ref, total, diagonal_ref, dfull, dpair, dhalf, dx, dquarter, dy, dz, dquarter2, dhalf2,
+    inverse_ref, total, diagonal_ref, dfull, dx, dquarter, dy, dz, dquarter2,
     load_sem, sib_send, sib_recv,
     fwd1_send, fwd1_recv, fin1_send, fin1_recv,
     fwd2_send, fwd2_recv, fin2_send, fin2_recv,
@@ -115,7 +113,7 @@
     row, col = lax.axis_index("row"), lax.axis_index("col")
     core = lax.rem(row, 2)
     place = (lax.div(row, 2), lax.div(col, 4), lax.rem(col, 4))
-    blocks = strip.shape[0]
+    blocks, items, width = strip_ref.shape[0], tile_ref.shape[0], strip_ref.shape[1]
 
     def device(y, x, z, c):
         return (y * 2 + c, x * 4 + z)
@@ -127,28 +125,41 @@
 
     sibling = device(*place, 1 - core)
 
+    def plane_peer(step, flip):
+        return device(
+            place[0], lax.rem(place[1] + step, 4), place[2], 1 - core if flip else core
+        )
+
+    around = [(step, flip) for step in range(4) for flip in (0, 1) if step or flip]
+
     barrier = pltpu.get_barrier_semaphore()
-    partners = [peer(a, s) for a in range(3) for s in (1, 2, 3)] + [sibling]
+    partners = [peer(a, s) for a in (0, 2) for s in (1, 2, 3)] + [plane_peer(*at) for at in around]
     for partner in partners:
         pl.semaphore_signal(barrier, inc=1, device_id=partner, device_id_type=MESH)
-    get_strip = pltpu.make_async_copy(strip_ref, strip, load_sem.at[0])
-    get_tile = pltpu.make_async_copy(tile_ref, tile, load_sem.at[1])
+    get_strip = pltpu.make_async_copy(strip_ref, strip.at[pl.ds(0, blocks)], load_sem.at[0])
+    get_tile = pltpu.make_async_copy(tile_ref, tile.at[pl.ds(0, items)], load_sem.at[1])
     get_strip.start()
     get_tile.start()
-    get_strip.wait()
-
-    left[blocks] = jnp.zeros(left.shape[1:], left.dtype)
-
-    def build(b, carry):
-        scaled = strip[b] * weight_ref[b]
-        high = scaled.astype(jnp.bfloat16).astype(F32)
-        low = scaled - high
-        stack = jnp.concatenate([high, high, low, low], axis=0)
-        left[b] = stack.T.astype(jnp.bfloat16)
-        return carry
-
-    lax.fori_loop(0, blocks, build, 0)
-    get_tile.wait()
+
+    lane = lax.broadcasted_iota(jnp.int32, (blocks, 128), 1)
+    block = lax.broadcasted_iota(jnp.int32, (blocks, 128), 0)
+    least = jnp.full((blocks, 128), items, jnp.int32)
+    most = jnp.full((blocks, 128), -1, jnp.int32)
+    for k in range(4):
+        listed = list_ref[:, k : k + 1] == lane
+        number = block * 4 + k
+        least = jnp.minimum(least, jnp.where(listed, number, items))
+        most = jnp.maximum(most, jnp.where(listed, number, -1))
+    least = jnp.min(least, axis=0, keepdims=True)
+    most = jnp.max(most, axis=0, keepdims=True)
+    slots[0, 0:1] = least
+    slots[0, 1:2] = jnp.where((most == least) | (most < 0), items, most)
+    own_table = pltpu.make_async_copy(slots.at[0], table.at[0], load_sem.at[2])
+    own_table.start()
+
+    column = lax.broadcasted_iota(jnp.int32, (width, blocks), 0)
+    lives[0] = jnp.zeros(lives.shape[1:], F32)
+    lives[0, :, :blocks] = jnp.where(column < count_ref[...], weight_ref[...].T, 0.0)
     pl.semaphore_wait(barrier, len(partners))
 
     def remote(src, dst, send, recv, to):
@@ -157,28 +168,58 @@
             device_id=to, device_id_type=MESH,
         )
 
-    def product(ty, tx, tz, c):
-        number = ((ty * 2 + c) * 4 + tx) * 4 + tz
+    def build(first, skip):
+        def body(q, carry):
+            for n in range(4):
+                b = first + 4 * q + n
+                high = scaled[b].astype(jnp.bfloat16).astype(F32)
+                low = scaled[b] - high
+                stack = jnp.concatenate([high, high, low, low], axis=0)
+                left[b + skip] = stack.T.astype(jnp.bfloat16)
+            return carry
+
+        lax.fori_loop(0, blocks // 4, body, 0)
+
+    def weigh(n):
+        live = lives[n]
+        for b in range(blocks):
+            scaled[n * blocks + b] = strip[n * blocks + b] * live[:, b : b + 1]
+
+    across = [
+        remote(src, dst, sib_send.at[n], sib_recv.at[n], sibling)
+        for n, (src, dst) in enumerate([
+            (lives.at[0], lives.at[1]),
+            (strip_ref, strip.at[pl.ds(blocks, blocks)]),
+            (slots.at[0], slots.at[1]),
+            (tile_ref, tile.at[pl.ds(items, items)]),
+        ])
+    ]
+    for copy in across:
+        copy.start()
+    zero = jnp.zeros(left.shape[1:], left.dtype)
+    left[blocks] = zero
+    left[2 * blocks + 1] = zero
+    get_strip.wait()
+    weigh(0)
+    build(0, 0)
+
+    def product(ty, tx, tz):
+        number = ((ty * 2 + core) * 4 + tx) * 4 + tz
         lefts, rights = [], []
-        for n in range(2):
-            slot = item_ref[2 * number + n]
-            lefts.append(left[lax.div(slot, 4)])
-            high, low = split(tile[lax.rem(slot, tile.shape[0])])
+        for n in range(4):
+            slot = table[n // 2, n % 2, number]
+            lefts.append(left[lax.div(slot, 4) + (n // 2) * (blocks + 1)])
+            high, low = split(tile[lax.rem(slot, items) + (n // 2) * items])
             rights += [high, low, high, low]
         return dot(jnp.concatenate(lefts, axis=1), jnp.concatenate(rights, axis=0))
 
     def offset(d):
         return jnp.where(d == 0, 2, jnp.where(d == 1, 1, jnp.where(d == 2, 3, 0)))
 
-    def group_tiles(i, c):
-        ty = lax.rem(place[0] + offset(lax.div(i, 4)), 4)
-        tx = lax.rem(place[1] + offset(lax.rem(i, 4)), 4)
-        return [functools.partial(product, ty, tx, lax.rem(place[2] + o, 4), c) for o in OFFSET]
-
-    def to_sibling(k):
-        return remote(
-            sent.at[lax.rem(k, RING)], acc.at[k], sib_send.at[k], sib_recv.at[k], sibling
-        )
+    def group_digits(i):
+        turn, at = lax.div(i, 4), lax.rem(i, 4)
+        y = jnp.where(at == 0, 0, jnp.where(at == 1, 3, at - 1))
+        return [(y, x, lax.rem(turn + 8 - y - x, 4)) for x in range(4)]
 
     def rows_of(p):
         return pl.ds(*ROWS[p])
@@ -201,136 +242,109 @@
             send.at[p, way, j], recv.at[p, way, j], peer(axis, 1 + 2 * way),
         )
 
-    def send_on(i, dz):
-        k = 4 * i + dz
-        digit = (lax.div(i, 4), lax.rem(i, 4), dz)
+    def send_on(k, digit):
         for p in range(3):
             da, db, dc = digit[p], digit[(p + 1) % 3], digit[(p + 2) % 3]
-            if p == 2 and dz == 3:
-                continue
-
-            if p != 2 or dz == 0:
-                @pl.when(da == 0)
-                def _():
-                    way = jnp.where(dc < 2, 0, 1)
-                    fwd_copy(1, p, way, k, db * 2 + lax.rem(dc, 2)).start()
-
-            if p != 2 or dz > 0:
-                @pl.when(((da == 1) & (dc >= 2)) | ((da == 2) & (dc < 2)))
-                def _():
-                    fin_copy(1, p, da - 1, k, db * 4 + dc).start()
-
-    def give_group(i, fresh=False):
-        for n, term in enumerate(group_tiles(i, 1 - core)):
-            sent[lax.rem(4 * i + n, RING)] = term()
-
-    def give(i, carry):
-        give_group(i)
-        for n in range(4):
-            to_sibling(4 * i + n).start()
-        return carry
-
-    def take_group(i):
-        for n, term in enumerate(group_tiles(i, core)):
-            acc[4 * i + n] = acc[4 * i + n] + term()
-
-    def take(i, carry):
-        for n in range(4):
-            to_sibling(4 * i + n).wait_recv()
-        take_group(i)
-        for n in range(4):
-            send_on(i, n)
-        return carry
-
-    def both(i, carry):
-        @pl.when(i >= RING // 4 - LAG)
-        def _():
-            for n in range(4):
-                to_sibling(4 * (i + LAG) - RING + n).wait_send()
-
-        for n in range(4):
-            to_sibling(4 * i + n).wait_recv()
-        give_group(i + LAG)
-        take_group(i)
-        for n in range(4):
-            to_sibling(4 * (i + LAG) + n).start()
-        for n in range(4):
-            send_on(i, n)
-
-        @pl.when(i == 3)
-        def _():
-            dfull[...] = jnp.zeros_like(dfull)
-            lax.fori_loop(0, blocks // 2, diagonal_local, 0)
-            d_start(0)
-
-        for phase, after in enumerate((5, 7, 9, 11, 13)):
+
+            if isinstance(da, int):
+                da = jnp.int32(da)
+
+            @pl.when(da == 0)
+            def _():
+                way = jnp.where(dc < 2, 0, 1)
+                fwd_copy(1, p, way, k, db * 2 + lax.rem(dc, 2)).start()
+
+            @pl.when(((da == 1) & (dc >= 2)) | ((da == 2) & (dc < 2)))
+            def _():
+                fin_copy(1, p, da - 1, k, db * 4 + dc).start()
+
+    def tiles(i, carry):
+        group = group_digits(i)
+        at = [y * 16 + x * 4 + z for y, x, z in group]
+        for k, digit in zip(at, group):
+            acc[k] = product(*[lax.rem(place[a] + offset(digit[a]), 4) for a in range(3)])
+        for k, digit in zip(at, group):
+            send_on(k, digit)
+        for phase, after in enumerate(TURNS):
             @pl.when(i == after)
             def _():
-                d_arrive(phase)
-                d_start(phase + 1)
+                d_arrive(phase + 1)
+                d_start(phase + 2)
 
         return carry
 
     def diagonal_local(b, carry):
         lefts, rights = [], []
-        for s in range(2):
-            lefts.append(left[2 * b + s])
-            high, low = split(strip[2 * b + s])
+        for n in range(2):
+            lefts.append(left[2 * b + n])
+            high, low = split(strip[2 * b + n])
             rights += [high, low, high, low]
         dfull[...] = dfull[...] + dot(
             jnp.concatenate(lefts, axis=1), jnp.concatenate(rights, axis=0)
         )
         return carry
 
+    py, px, pz = place
+    mine = pl.ds(pl.multiple_of(64 * px + 32 * core, 32), 32)
+
     def d_copies(phase):
-        py, px, pz = place
-        if phase == 0:
-            return [remote(dfull.at[pl.ds(128 * (1 - core), 128)], dpair, d_send.at[0, 0], d_recv.at[0, 0], sibling)]
-        if phase == 6:
-            return [remote(dhalf2, diagonal_ref.at[pl.ds(128 * core, 128)], d_send.at[6, 0], d_recv.at[6, 0], sibling)]
         out = []
+        if phase in (0, 4):
+            for n, (step, flip) in enumerate(around):
+                there = 2 * lax.rem(px + step, 4) + (1 - core if flip else core)
+                if phase == 0:
+                    src, dst = dfull.at[pl.ds(pl.multiple_of(32 * there, 32), 32)], dx.at[n]
+                else:
+                    src = dst = diagonal_ref.at[mine]
+                out.append(remote(src, dst, d_send.at[phase, n], d_recv.at[phase, n], plane_peer(step, flip)))
+            return out
         for o in (1, 2, 3):
             if phase == 1:
-                src, dst, axis = dhalf.at[pl.ds(32 * lax.rem(px + o, 4), 32)], dx.at[o - 1], 1
+                src, dst, axis = dquarter.at[pl.ds(8 * lax.rem(py + o, 4), 8)], dy.at[o - 1], 0
             elif phase == 2:
-                src, dst, axis = dquarter.at[pl.ds(8 * lax.rem(py + o, 4), 8)], dy.at[o - 1], 0
-            elif phase == 3:
                 src, dst, axis = dz.at[pz], dz.at[pz], 2
-            elif phase == 4:
+            else:
                 part = pl.ds(8 * py, 8)
                 src, dst, axis = dquarter2.at[part], dquarter2.at[part], 0
-            else:
-                part = pl.ds(32 * px, 32)
-                src, dst, axis = dhalf2.at[part], dhalf2.at[part], 1
             out.append(remote(src, dst, d_send.at[phase, o - 1], d_recv.at[phase, o - 1], peer(axis, o)))
         return out
 
     def d_arrive(phase):
-        py, px, pz = place
-        for o, copy in enumerate(d_copies(phase)):
+        for copy in d_copies(phase):
             copy.wait_recv()
         if phase == 0:
-            dhalf[...] = dfull[pl.ds(128 * core, 128)] + dpair[...]
+            held = dfull[mine]
+            for n in range(len(around)):
+                held = held + dx[n]
+            dquarter[...] = held
         elif phase == 1:
-            dquarter[...] = dhalf[pl.ds(32 * px, 32)] + dx[0] + dx[1] + dx[2]
+            dz[pz] = dquarter[pl.ds(8 * py, 8)] + dy[0] + dy[1] + dy[2]
         elif phase == 2:
-            dz[pz] = dquarter[pl.ds(8 * py, 8)] + dy[0] + dy[1] + dy[2]
+            dquarter2[pl.ds(8 * py, 8)] = dz[0] + dz[1] + dz[2] + dz[3]
         elif phase == 3:
-            dquarter2[pl.ds(8 * py, 8)] = dz[0] + dz[1] + dz[2] + dz[3]
-        elif phase == 4:
-            dhalf2[pl.ds(32 * px, 32)] = dquarter2[...]
-        elif phase == 5:
-            diagonal_ref[pl.ds(128 * core, 128)] = dhalf2[...]
+            diagonal_ref[mine] = dquarter2[...]
 
     def d_start(phase):
         for copy in d_copies(phase):
             copy.start()
 
-    lax.fori_loop(0, LAG, give, 0)
-    lax.fori_loop(0, 16 - LAG, both, 0)
-    lax.fori_loop(16 - LAG, 16, take, 0)
-    d_arrive(5)
-    d_start(6)
+    dfull[...] = jnp.zeros_like(dfull)
+    lax.fori_loop(0, blocks // 2, diagonal_local, 0)
+    d_start(0)
+    across[0].wait_recv()
+    across[1].wait_recv()
+    weigh(1)
+    build(blocks, 1)
+    across[2].wait_recv()
+    their_table = pltpu.make_async_copy(slots.at[1], table.at[1], load_sem.at[3])
+    their_table.start()
+    d_arrive(0)
+    d_start(1)
+    own_table.wait()
+    their_table.wait()
+    get_tile.wait()
+    across[3].wait_recv()
+    lax.fori_loop(0, 16, tiles, 0)
 
     def slot(p, da, db, dc):
         digit = [0, 0, 0]
@@ -417,7 +431,7 @@
                     fin3_copy(p, way, half).wait_recv()
             total[rows_of(p)] = acc[63, rows_of(p)] + fin3[p][0] + fin3[p][1]
 
-    d_arrive(6)
+    d_arrive(4)
     moves = {PACE * (f + 1): functools.partial(gather1, f) for f in range(16)}
     moves |= {SECOND[j]: functools.partial(pass2, j) for j in range(2)}
     moves |= {SECOND[2 + dc]: functools.partial(gather2, dc) for dc in range(4)}
@@ -432,12 +446,9 @@
     gather3()
     update_ref[...] = full_dot(inverse_ref[...], total[...])
 
-    def drain_ring(k, carry):
-        to_sibling(k).wait_send()
-        return carry
-
-    lax.fori_loop(64 - RING, 64, drain_ring, 0)
-    for phase in range(7):
+    for copy in across:
+        copy.wait_send()
+    for phase in range(5):
         for copy in d_copies(phase):
             copy.wait_send()
 
@@ -465,7 +476,7 @@
             fwd3_copy(p, way).wait_send()
 
 
-def gather_and_sum(item, weight, strip_columns, tiles):
+def gather_and_sum(weight, count, lists, strip_columns, tiles):
     blocks, width, rows = strip_columns.shape
     items = tiles.shape[0]
     dma = pltpu.SemaphoreType.DMA
@@ -476,49 +487,40 @@
     return pl.pallas_call(
         kernel,
         out_shape=[jax.ShapeDtypeStruct((256, 256), F32)] * 2,
-        in_specs=[pl.BlockSpec(memory_space=pltpu.SMEM), in_vmem, any_space, any_space],
+        in_specs=[in_vmem, in_vmem, in_vmem, any_space, any_space],
         out_specs=[in_vmem, in_vmem],
         scratch_shapes=[
-            vmem(blocks, width, rows), vmem(items, width, rows),
-            pltpu.VMEM((blocks + 1, rows, 4 * width), jnp.bfloat16),
-            vmem(RING, 256, 256), vmem(64, 256, 256),
+            vmem(2 * blocks, width, rows), vmem(2 * blocks, width, rows),
+            vmem(2 * items, width, rows),
+            pltpu.VMEM((2 * blocks + 2, rows, 4 * width), jnp.bfloat16),
+            vmem(2, width, 128), pltpu.VMEM((2, 2, 128), jnp.int32), pltpu.SMEM((2, 2, 128), jnp.int32),
+            vmem(64, 256, 256),
             *[vmem(2, 8, s, 256) for s in sizes], *[vmem(2, 16, s, 256) for s in sizes],
             *[vmem(2, 2, s, 256) for s in sizes], *[vmem(2, 4, s, 256) for s in sizes],
             *[vmem(2, CUT, 256) for s in sizes], *[vmem(2, s, 256) for s in sizes],
             vmem(256, 256), vmem(256, 256), vmem(256, 256),
-            vmem(256, 256), vmem(128, 256), vmem(128, 256), vmem(3, 32, 256), vmem(32, 256),
-            vmem(3, 8, 256), vmem(4, 8, 256), vmem(32, 256), vmem(128, 256),
-            dma((2,)), dma((64,)), dma((64,)),
+            vmem(256, 256), vmem(7, 32, 256), vmem(32, 256),
+            vmem(3, 8, 256), vmem(4, 8, 256), vmem(32, 256),
+            dma((4,)), dma((4,)), dma((4,)),
             dma((3, 2, 8)), dma((3, 2, 8)), dma((3, 2, 16)), dma((3, 2, 16)),
             dma((3, 2, 2)), dma((3, 2, 2)), dma((3, 2, 4)), dma((3, 2, 4)),
             dma((3, 2)), dma((3, 2)), dma((3, 2, 2)), dma((3, 2, 2)),
-            dma((7, 3)), dma((7, 3)),
+            dma((5, 7)), dma((5, 7)),
         ],
         compiler_params=pltpu.CompilerParams(
             collective_id=0, has_side_effects=True, vmem_limit_bytes=60 << 20
         ),
-    )(item, weight, strip_columns, tiles)
+    )(weight, count, lists, strip_columns, tiles)
 
 
 def per_device(strip_columns, tile_columns, barrier_weights, column_counts, tile_lists):
-    blocks, width, rows = strip_columns.shape
-    touched = tile_columns.shape[1]
-    own_width = tile_columns.shape[3]
-    devices = lax.axis_size(AXES)
-    items = blocks * touched
-    live_mask = jnp.arange(width, dtype=jnp.int32)[None, :] < column_counts[:, None]
-    live_weight = jnp.where(live_mask, barrier_weights, 0.0)
-    listed = tile_lists.reshape(1, items) == jnp.arange(devices, dtype=jnp.int32)[:, None]
-    number = jnp.arange(items, dtype=jnp.int32)[None, :]
-    least = jnp.min(jnp.where(listed, number, items), axis=1)
-    most = jnp.max(jnp.where(listed, number, -1), axis=1)
-    most = jnp.where((most == least) | (most < 0), items, most)
-    slot = jnp.stack([least, most], axis=1).reshape(devices * 2)
+    blocks, touched, width, own_width = tile_columns.shape
     return gather_and_sum(
-        slot,
-        live_weight[:, :, None],
+        barrier_weights,
+        column_counts.reshape(1, blocks),
+        tile_lists,
         strip_columns,
-        tile_columns.reshape(items, width, own_width),
+        tile_columns.reshape(blocks * touched, width, own_width),
     )
 
 

time: 118 us -> 99 us (0.84); the launches traced: 116 us -> 98.7 us
  Pallas kernels: 109 us -> 93.4 us
  local copies, waits for them, and re-layouts: 6.08 us -> 4.71 us
    pallas_call x1, Pallas kernels: 109 us -> 93.4 us  [gather_and_sum(): pl.pallas_call(kernel, out_shape=[jax.ShapeDtypeStruct((256, 256), F32)]...]
where the time goes in v3:
time: 99 us; the launch traced here: 98.7 us
  Pallas kernels  93.4 us (94%)
  local copies, waits for them, and re-layouts  4.71 us (5%)
    pallas_call x1, Pallas kernels, gather_and_sum(): pl.pallas_call(kernel, out_shape=[jax.ShapeDtypeStruct((256, 256), F32)]...  93.4 us
    unnamed x3, local copies, waits for them, and re-layouts  4.71 us

profile of v3, /device:TPU:0, one launch (start us, length us, event | category | flops | bytes accessed | tf_op | source)
XLA Modules:
  0.0 98.7 jit_solution(8212309804959030330)
XLA Ops:
  0.6 1.4 %copy.7.list_ref = s32[32,4]{1,0:T(8,128)} copy(s32[32,4]{0,1:T(4,128)} %param.9) | data formatting | bytes 1024 | tf_op args[4]
  2.0 93.4 %shard_map.68 = (f32[256,256]{1,0:T(8,128)}, f32[256,256]{1,0:T(8,128)}) custom-call(f32[32,32]{1,0:T(8,128)} %weight_ref.1, s32[1,32]{1,0:T(1,128)} %bitcast.3, s32[32,4]{1,0:T(8,128)} %copy.7.list_ref, f32[32,32,256]{2,1,0:T(8,128)} %strip_ref.1, f32[128,32,256]{2,1,0:T(8,128)} %bitcast.2), custom_call_target="tpu_custom_call" | custom-call | tf_op jit(solution)/shard_map/pallas_call | solution.py:487
  95.4 1.7 %copy.10 = f32[256,256]{1,0:T(8,128)} copy(f32[256,256]{1,0:T(8,128)} %get-tuple-element.4) | data formatting | bytes 524288
  97.1 1.7 %copy.11 = f32[256,256]{1,0:T(8,128)} copy(f32[256,256]{1,0:T(8,128)} %get-tuple-element.5) | data formatting | bytes 524288

commit v4 on v3

--- a/solution.py
+++ b/solution.py
@@ -9,8 +9,10 @@
 
 AXES = ("row", "col")
 MESH = pl.DeviceIdType.MESH
-ROWS = ((0, 88), (88, 88), (176, 80))
-CUT = 48
+ROWS = ((0, 88), (88, 80), (168, 88))
+CUT = 40
+PASS = (0, 3, 4, 7, 1, 2, 5, 6)
+ORDER = tuple(4 * (j // 2) + j % 2 + 2 * way for j in PASS for way in range(2))
 TURNS = (1, 4, 8)
 PACE = 5
 SECOND = (88, 92, 100, 106, 112, 118, 126)
@@ -95,21 +97,14 @@
 
 
 def kernel(
-    weight_ref, count_ref, list_ref, strip_ref, tile_ref, factor_ref, update_ref,
+    weight_ref, count_ref, list_ref, strip_ref, tile_ref, factor_ref, inverse_ref, sum_ref,
     strip, scaled, tile, left, lives, slots, table, acc,
-    fwd10, fwd11, fwd12, fin10, fin11, fin12,
-    fwd20, fwd21, fwd22, fin20, fin21, fin22,
-    fwd30, fwd31, fwd32, fin30, fin31, fin32,
-    inverse_ref, total, diagonal_ref, dfull, dx, dquarter, dy, dz, dquarter2,
+    fwd1, fin1, fwd2, fin2, fwd3, fin3,
+    diagonal_ref, dfull, dx, dquarter, dy, dz, dquarter2,
     load_sem, sib_send, sib_recv,
-    fwd1_send, fwd1_recv, fin1_send, fin1_recv,
-    fwd2_send, fwd2_recv, fin2_send, fin2_recv,
-    fwd3_send, fwd3_recv, fin3_send, fin3_recv,
+    fwd1_recv, fin1_recv, fwd2_recv, fin2_recv, out_send, last_recv,
     d_send, d_recv,
 ):
-    fwd1, fin1 = (fwd10, fwd11, fwd12), (fin10, fin11, fin12)
-    fwd2, fin2 = (fwd20, fwd21, fwd22), (fin20, fin21, fin22)
-    fwd3, fin3 = (fwd30, fwd31, fwd32), (fin30, fin31, fin32)
     row, col = lax.axis_index("row"), lax.axis_index("col")
     core = lax.rem(row, 2)
     place = (lax.div(row, 2), lax.div(col, 4), lax.rem(col, 4))
@@ -145,8 +140,9 @@
     block = lax.broadcasted_iota(jnp.int32, (blocks, 128), 0)
     least = jnp.full((blocks, 128), items, jnp.int32)
     most = jnp.full((blocks, 128), -1, jnp.int32)
+    lists = list_ref[...].T
     for k in range(4):
-        listed = list_ref[:, k : k + 1] == lane
+        listed = lists[:, k : k + 1] == lane
         number = block * 4 + k
         least = jnp.minimum(least, jnp.where(listed, number, items))
         most = jnp.maximum(most, jnp.where(listed, number, -1))
@@ -225,22 +221,24 @@
         return pl.ds(*ROWS[p])
 
     def fwd_copy(stage, p, way, k, j):
-        fwd = (fwd1, fwd2)[stage - 1]
-        send, recv = ((fwd1_send, fwd1_recv), (fwd2_send, fwd2_recv))[stage - 1]
-        axis = (p + stage - 1) % 3
+        fwd, recv = ((fwd1, fwd1_recv), (fwd2, fwd2_recv))[stage - 1]
         return remote(
-            acc.at[k, rows_of(p)], fwd[p].at[way, j],
-            send.at[p, way, j], recv.at[p, way, j], peer(axis, 1 + 2 * way),
+            acc.at[k, rows_of(p)], fwd.at[way, j, rows_of(p)],
+            out_send.at[2 * stage - 2], recv.at[j], peer((p + stage - 1) % 3, 1 + 2 * way),
         )
 
     def fin_copy(stage, p, way, k, j):
-        fin = (fin1, fin2)[stage - 1]
-        send, recv = ((fin1_send, fin1_recv), (fin2_send, fin2_recv))[stage - 1]
-        axis = (p + stage - 1) % 3
+        fin, recv = ((fin1, fin1_recv), (fin2, fin2_recv))[stage - 1]
         return remote(
-            acc.at[k, rows_of(p)], fin[p].at[way, j],
-            send.at[p, way, j], recv.at[p, way, j], peer(axis, 1 + 2 * way),
-        )
+            acc.at[k, rows_of(p)], fin.at[way, j, rows_of(p)],
+            out_send.at[2 * stage - 1], recv.at[j], peer((p + stage - 1) % 3, 1 + 2 * way),
+        )
+
+    def all_here(buffer, recv):
+        remote(buffer, buffer, out_send.at[0], recv, sibling).wait_recv()
+
+    def all_gone(buffer, send):
+        remote(buffer, buffer, send, last_recv.at[0], sibling).wait_send()
 
     def send_on(k, digit):
         for p in range(3):
@@ -296,7 +294,7 @@
                     src, dst = dfull.at[pl.ds(pl.multiple_of(32 * there, 32), 32)], dx.at[n]
                 else:
                     src = dst = diagonal_ref.at[mine]
-                out.append(remote(src, dst, d_send.at[phase, n], d_recv.at[phase, n], plane_peer(step, flip)))
+                out.append(remote(src, dst, d_send.at[phase], d_recv.at[phase], plane_peer(step, flip)))
             return out
         for o in (1, 2, 3):
             if phase == 1:
@@ -306,12 +304,14 @@
             else:
                 part = pl.ds(8 * py, 8)
                 src, dst, axis = dquarter2.at[part], dquarter2.at[part], 0
-            out.append(remote(src, dst, d_send.at[phase, o - 1], d_recv.at[phase, o - 1], peer(axis, o)))
+            out.append(remote(src, dst, d_send.at[phase], d_recv.at[phase], peer(axis, o)))
         return out
 
+    def d_bytes(phase):
+        return (dx, dy, dz.at[pl.ds(0, 3)], dquarter2.at[pl.ds(0, 24)], diagonal_ref.at[pl.ds(0, 224)])[phase]
+
     def d_arrive(phase):
-        for copy in d_copies(phase):
-            copy.wait_recv()
+        all_here(d_bytes(phase), d_recv.at[phase])
         if phase == 0:
             held = dfull[mine]
             for n in range(len(around)):
@@ -351,35 +351,36 @@
         digit[p], digit[(p + 1) % 3], digit[(p + 2) % 3] = da, db, dc
         return digit[0] * 16 + digit[1] * 4 + digit[2]
 
-    for j in range(8):
+    for j in PASS:
         db = j // 2
+        all_here(fwd1.at[:, j], fwd1_recv.at[j])
         for p in range(3):
             for way in range(2):
                 dc = j % 2 + 2 * way
                 k = slot(p, 1 + way, db, dc)
-                fwd_copy(1, p, way, k, j).wait_recv()
-                acc[k, rows_of(p)] = acc[k, rows_of(p)] + fwd1[p][way, j]
+                acc[k, rows_of(p)] = acc[k, rows_of(p)] + fwd1[way, j, rows_of(p)]
                 fin_copy(1, p, way, k, db * 4 + dc).start()
+
     def gather1(f):
         db, dc = f // 4, f % 4
+        all_here(fin1.at[:, f], fin1_recv.at[f])
         for p in range(3):
             k = slot(p, 3, db, dc)
-            for way in range(2):
-                fin_copy(1, p, way, k, f).wait_recv()
-            acc[k, rows_of(p)] = acc[k, rows_of(p)] + fin1[p][0, f] + fin1[p][1, f]
+            acc[k, rows_of(p)] = acc[k, rows_of(p)] + fin1[0, f, rows_of(p)] + fin1[1, f, rows_of(p)]
             if db == 0:
                 fwd_copy(2, p, dc // 2, k, dc % 2).start()
             if db == 1 and dc >= 2:
                 fin_copy(2, p, 0, k, dc).start()
             if db == 2 and dc < 2:
                 fin_copy(2, p, 1, k, dc).start()
+
     def pass2(j):
+        all_here(fwd2.at[:, j], fwd2_recv.at[j])
         for p in range(3):
             for way in range(2):
                 dc = j + 2 * way
                 k = slot(p, 3, 1 + way, dc)
-                fwd_copy(2, p, way, k, j).wait_recv()
-                acc[k, rows_of(p)] = acc[k, rows_of(p)] + fwd2[p][way, j]
+                acc[k, rows_of(p)] = acc[k, rows_of(p)] + fwd2[way, j, rows_of(p)]
                 fin_copy(2, p, way, k, dc).start()
 
     def part3(p, way):
@@ -387,27 +388,24 @@
         return (low, CUT) if way == 0 else (low + CUT, size - CUT)
 
     def fwd3_copy(p, way):
-        low, size = part3(p, way)
+        rows = pl.ds(*part3(p, way))
         return remote(
-            acc.at[slot(p, 3, 3, 0), pl.ds(low, size)], fwd3[p].at[way, pl.ds(0, size)],
-            fwd3_send.at[p, way], fwd3_recv.at[p, way], peer((p + 2) % 3, (1, 3)[way]),
+            acc.at[slot(p, 3, 3, 0), rows], fwd3.at[rows],
+            out_send.at[4], last_recv.at[0], peer((p + 2) % 3, 1 + 2 * way),
         )
 
     def fin3_copy(p, way, half):
-        low, size = part3(p, half)
+        rows = pl.ds(*part3(p, half))
         return remote(
-            acc.at[slot(p, 3, 3, 1 + way), pl.ds(low, size)],
-            fin3[p].at[way, pl.ds(low - ROWS[p][0], size)],
-            fin3_send.at[p, way, half], fin3_recv.at[p, way, half],
-            peer((p + 2) % 3, (1, 3)[way]),
+            acc.at[slot(p, 3, 3, 1 + way), rows], fin3.at[way, rows],
+            out_send.at[5], last_recv.at[1], peer((p + 2) % 3, 1 + 2 * way),
         )
 
     def gather2(dc):
+        all_here(fin2.at[:, dc], fin2_recv.at[dc])
         for p in range(3):
             k = slot(p, 3, 3, dc)
-            for way in range(2):
-                fin_copy(2, p, way, k, dc).wait_recv()
-            acc[k, rows_of(p)] = acc[k, rows_of(p)] + fin2[p][0, dc] + fin2[p][1, dc]
+            acc[k, rows_of(p)] = acc[k, rows_of(p)] + fin2[0, dc, rows_of(p)] + fin2[1, dc, rows_of(p)]
             if dc == 0:
                 fwd3_copy(p, 0).start()
                 fwd3_copy(p, 1).start()
@@ -415,24 +413,22 @@
                 fin3_copy(p, 0, 1).start()
             if dc == 2:
                 fin3_copy(p, 1, 0).start()
+
     def pass3():
+        all_here(fwd3, last_recv.at[0])
         for p in range(3):
             for way in range(2):
-                low, size = part3(p, way)
+                rows = pl.ds(*part3(p, way))
                 k = slot(p, 3, 3, 1 + way)
-                fwd3_copy(p, way).wait_recv()
-                acc[k, pl.ds(low, size)] = acc[k, pl.ds(low, size)] + fwd3[p][way, pl.ds(0, size)]
+                acc[k, rows] = acc[k, rows] + fwd3[rows]
                 fin3_copy(p, way, way).start()
 
     def gather3():
-        for p in range(3):
-            for way in range(2):
-                for half in range(2):
-                    fin3_copy(p, way, half).wait_recv()
-            total[rows_of(p)] = acc[63, rows_of(p)] + fin3[p][0] + fin3[p][1]
+        all_here(fin3, last_recv.at[1])
+        sum_ref[...] = acc[63] + fin3[0] + fin3[1]
 
     d_arrive(4)
-    moves = {PACE * (f + 1): functools.partial(gather1, f) for f in range(16)}
+    moves = {PACE * (n + 1): functools.partial(gather1, f) for n, f in enumerate(ORDER)}
     moves |= {SECOND[j]: functools.partial(pass2, j) for j in range(2)}
     moves |= {SECOND[2 + dc]: functools.partial(gather2, dc) for dc in range(4)}
     moves[SECOND[6]] = pass3
@@ -444,36 +440,18 @@
     for step in sorted(moves):
         moves[step]()
     gather3()
-    update_ref[...] = full_dot(inverse_ref[...], total[...])
 
     for copy in across:
         copy.wait_send()
     for phase in range(5):
-        for copy in d_copies(phase):
-            copy.wait_send()
-
-    def drain(i, carry):
-        for p in range(3):
-            for way in range(2):
-                fin_copy(1, p, way, 0, i).wait_send()
-        return carry
-
-    def drain_half(i, carry):
-        for p in range(3):
-            for way in range(2):
-                fwd_copy(1, p, way, 0, i).wait_send()
-        return carry
-
-    lax.fori_loop(0, 16, drain, 0)
-    lax.fori_loop(0, 8, drain_half, 0)
-    for p in range(3):
-        for way in range(2):
-            for j in range(2):
-                fwd_copy(2, p, way, 0, j).wait_send()
-                fin3_copy(p, way, j).wait_send()
-            for j in range(4):
-                fin_copy(2, p, way, 0, j).wait_send()
-            fwd3_copy(p, way).wait_send()
+        all_gone(d_bytes(phase), d_send.at[phase])
+    for n, buffer in enumerate((fwd1, fin1, fwd2, fin2, fwd3, fin3)):
+        all_gone(buffer, out_send.at[n])
+
+
+def finish(factor_ref, inverse_ref, sum_ref, factor_out, update_out):
+    factor_out[...] = factor_ref[...]
+    update_out[...] = full_dot(inverse_ref[...], sum_ref[...])
 
 
 def gather_and_sum(weight, count, lists, strip_columns, tiles):
@@ -481,31 +459,27 @@
     items = tiles.shape[0]
     dma = pltpu.SemaphoreType.DMA
     vmem = lambda *shape: pltpu.VMEM(shape, F32)
-    sizes = [size for _, size in ROWS]
     any_space = pl.BlockSpec(memory_space=pl.ANY)
     in_vmem = pl.BlockSpec(memory_space=pltpu.VMEM)
     return pl.pallas_call(
         kernel,
-        out_shape=[jax.ShapeDtypeStruct((256, 256), F32)] * 2,
+        out_shape=[jax.ShapeDtypeStruct((256, 256), F32)] * 3,
         in_specs=[in_vmem, in_vmem, in_vmem, any_space, any_space],
-        out_specs=[in_vmem, in_vmem],
+        out_specs=[in_vmem] * 3,
         scratch_shapes=[
             vmem(2 * blocks, width, rows), vmem(2 * blocks, width, rows),
             vmem(2 * items, width, rows),
             pltpu.VMEM((2 * blocks + 2, rows, 4 * width), jnp.bfloat16),
             vmem(2, width, 128), pltpu.VMEM((2, 2, 128), jnp.int32), pltpu.SMEM((2, 2, 128), jnp.int32),
             vmem(64, 256, 256),
-            *[vmem(2, 8, s, 256) for s in sizes], *[vmem(2, 16, s, 256) for s in sizes],
-            *[vmem(2, 2, s, 256) for s in sizes], *[vmem(2, 4, s, 256) for s in sizes],
-            *[vmem(2, CUT, 256) for s in sizes], *[vmem(2, s, 256) for s in sizes],
-            vmem(256, 256), vmem(256, 256), vmem(256, 256),
+            vmem(2, 8, 256, 256), vmem(2, 16, 256, 256), vmem(2, 2, 256, 256), vmem(2, 4, 256, 256),
+            vmem(256, 256), vmem(2, 256, 256),
+            vmem(256, 256),
             vmem(256, 256), vmem(7, 32, 256), vmem(32, 256),
             vmem(3, 8, 256), vmem(4, 8, 256), vmem(32, 256),
             dma((4,)), dma((4,)), dma((4,)),
-            dma((3, 2, 8)), dma((3, 2, 8)), dma((3, 2, 16)), dma((3, 2, 16)),
-            dma((3, 2, 2)), dma((3, 2, 2)), dma((3, 2, 4)), dma((3, 2, 4)),
-            dma((3, 2)), dma((3, 2)), dma((3, 2, 2)), dma((3, 2, 2)),
-            dma((5, 7)), dma((5, 7)),
+            dma((8,)), dma((16,)), dma((2,)), dma((4,)), dma((6,)), dma((2,)),
+            dma((5,)), dma((5,)),
         ],
         compiler_params=pltpu.CompilerParams(
             collective_id=0, has_side_effects=True, vmem_limit_bytes=60 << 20
@@ -515,13 +489,20 @@
 
 def per_device(strip_columns, tile_columns, barrier_weights, column_counts, tile_lists):
     blocks, touched, width, own_width = tile_columns.shape
-    return gather_and_sum(
+    in_vmem = pl.BlockSpec(memory_space=pltpu.VMEM)
+    parts = gather_and_sum(
         barrier_weights,
         column_counts.reshape(1, blocks),
-        tile_lists,
+        tile_lists.T,
         strip_columns,
         tile_columns.reshape(blocks * touched, width, own_width),
     )
+    return pl.pallas_call(
+        finish,
+        out_shape=[jax.ShapeDtypeStruct((256, 256), F32)] * 2,
+        in_specs=[in_vmem] * 3,
+        out_specs=[in_vmem] * 2,
+    )(*parts)
 
 
 def solution(mesh):

time: 99 us -> 92 us (0.929)
  local copies, waits for them, and re-layouts: 4.71 us -> 0 us
  Pallas kernels: 93.4 us -> 91.2 us
    unnamed x3 -> x0, local copies, waits for them, and re-layouts: 4.71 us -> none
    pallas_call x1, Pallas kernels: 93.4 us -> 89 us  [gather_and_sum(): pl.pallas_call(kernel, out_shape=[jax.ShapeDtypeStruct((256, 256), F32)]...]
    pallas_call x0 -> x1, Pallas kernels: none -> 2.22 us  [per_device(): pl.pallas_call(finish, out_shape=[jax.ShapeDtypeStruct((256, 256), F32)]...]
where the time goes in v4:
time: 92 us; the launch traced here: 91.8 us
  Pallas kernels  91.2 us (99%)
    pallas_call x1, Pallas kernels, gather_and_sum(): pl.pallas_call(kernel, out_shape=[jax.ShapeDtypeStruct((256, 256), F32)]...  89 us
    pallas_call x1, Pallas kernels, per_device(): pl.pallas_call(finish, out_shape=[jax.ShapeDtypeStruct((256, 256), F32)]...  2.22 us

profile of v4, /device:TPU:0, one launch (start us, length us, event | category | flops | bytes accessed | tf_op | source)
XLA Modules:
  0.0 91.8 jit_solution(18049406147868128444)
XLA Ops:
  0.6 89.0 %shard_map.68 = (f32[256,256]{1,0:T(8,128)}, f32[256,256]{1,0:T(8,128)}, f32[256,256]{1,0:T(8,128)}) custom-call(f32[32,32]{1,0:T(8,128)} %weight_ref.1, s32[1,32]{1,0:T(1,128)} %bitcast.5, s32[4,32]{1,0:T(4,128)} %bitcast.4, f32[32,32,256]{2,1,0:T(8,128)} %strip_ref.1, f32[128,32,256]{2,1,0:T(8,128)} %bitcast.3), custom_call_target="tpu_custom_call" | custom-call | tf_op jit(solution)/shard_map/pallas_call | solution.py:464
  89.6 2.2 %shard_map.69 = (f32[256,256]{1,0:T(8,128)}, f32[256,256]{1,0:T(8,128)}) custom-call(f32[256,256]{1,0:T(8,128)} %get-tuple-element.5.factor_ref, f32[256,256]{1,0:T(8,128)} %get-tuple-element.6.inverse_ref, f32[256,256]{1,0:T(8,128)} %get-tuple-element.7.sum_ref), custom_call_target="tpu_custom_call" | custom-call | tf_op jit(solution)/shard_map/pallas_call | solution.py:500

commit v5 on v4

--- a/solution.py
+++ b/solution.py
@@ -14,8 +14,8 @@
 PASS = (0, 3, 4, 7, 1, 2, 5, 6)
 ORDER = tuple(4 * (j // 2) + j % 2 + 2 * way for j in PASS for way in range(2))
 TURNS = (1, 4, 8)
-PACE = 5
-SECOND = (88, 92, 100, 106, 112, 118, 126)
+EARLY = 4
+WHEN = (24, 30, 36, 42, 50, 55, 60, 65, 70, 75, 80, 85, 90, 95, 100, 105, 110, 115, 120, 125)
 STRIDE = (16, 4, 1)
 F32 = jnp.float32
 
@@ -214,7 +214,7 @@
 
     def group_digits(i):
         turn, at = lax.div(i, 4), lax.rem(i, 4)
-        y = jnp.where(at == 0, 0, jnp.where(at == 1, 3, at - 1))
+        y = jnp.where(at == 1, 2, jnp.where(at == 2, 1, at))
         return [(y, x, lax.rem(turn + 8 - y - x, 4)) for x in range(4)]
 
     def rows_of(p):
@@ -351,7 +351,7 @@
         digit[p], digit[(p + 1) % 3], digit[(p + 2) % 3] = da, db, dc
         return digit[0] * 16 + digit[1] * 4 + digit[2]
 
-    for j in PASS:
+    def pass1(j):
         db = j // 2
         all_here(fwd1.at[:, j], fwd1_recv.at[j])
         for p in range(3):
@@ -427,19 +427,22 @@
         all_here(fin3, last_recv.at[1])
         sum_ref[...] = acc[63] + fin3[0] + fin3[1]
 
+    events = [functools.partial(pass1, j) for j in PASS]
+    events += [functools.partial(gather1, f) for f in ORDER]
+    events += [functools.partial(pass2, j) for j in range(2)]
+    events += [functools.partial(gather2, dc) for dc in range(4)]
+    events += [pass3, gather3]
+    for event in events[:EARLY]:
+        event()
     d_arrive(4)
-    moves = {PACE * (n + 1): functools.partial(gather1, f) for n, f in enumerate(ORDER)}
-    moves |= {SECOND[j]: functools.partial(pass2, j) for j in range(2)}
-    moves |= {SECOND[2 + dc]: functools.partial(gather2, dc) for dc in range(4)}
-    moves[SECOND[6]] = pass3
+    moves = dict(zip(WHEN, events[EARLY:]))
     step = 0
     for _ in factorize(diagonal_ref, factor_ref, inverse_ref):
         step += 1
         if step in moves:
             moves.pop(step)()
-    for step in sorted(moves):
-        moves[step]()
-    gather3()
+    for event in events[EARLY + len(WHEN) - len(moves) :]:
+        event()
 
     for copy in across:
         copy.wait_send()

time: 92 us -> 89.3 us (0.971)
  Pallas kernels: 91.2 us -> 88.4 us
    pallas_call x1, Pallas kernels: 89 us -> 86.2 us  [gather_and_sum(): pl.pallas_call(kernel, out_shape=[jax.ShapeDtypeStruct((256, 256), F32)]...]
where the time goes in v5:
time: 89.3 us; the launch traced here: 89.1 us
  Pallas kernels  88.4 us (99%)
    pallas_call x1, Pallas kernels, gather_and_sum(): pl.pallas_call(kernel, out_shape=[jax.ShapeDtypeStruct((256, 256), F32)]...  86.2 us
    pallas_call x1, Pallas kernels, per_device(): pl.pallas_call(finish, out_shape=[jax.ShapeDtypeStruct((256, 256), F32)]...  2.22 us

profile of v5, /device:TPU:0, one launch (start us, length us, event | category | flops | bytes accessed | tf_op | source)
XLA Modules:
  0.0 89.1 jit_solution(3748511611599280401)
XLA Ops:
  0.6 86.2 %shard_map.68 = (f32[256,256]{1,0:T(8,128)}, f32[256,256]{1,0:T(8,128)}, f32[256,256]{1,0:T(8,128)}) custom-call(f32[32,32]{1,0:T(8,128)} %weight_ref.1, s32[1,32]{1,0:T(1,128)} %bitcast.5, s32[4,32]{1,0:T(4,128)} %bitcast.4, f32[32,32,256]{2,1,0:T(8,128)} %strip_ref.1, f32[128,32,256]{2,1,0:T(8,128)} %bitcast.3), custom_call_target="tpu_custom_call" | custom-call | tf_op jit(solution)/shard_map/pallas_call | solution.py:467
  86.9 2.2 %shard_map.69 = (f32[256,256]{1,0:T(8,128)}, f32[256,256]{1,0:T(8,128)}) custom-call(f32[256,256]{1,0:T(8,128)} %get-tuple-element.5.factor_ref, f32[256,256]{1,0:T(8,128)} %get-tuple-element.6.inverse_ref, f32[256,256]{1,0:T(8,128)} %get-tuple-element.7.sum_ref), custom_call_target="tpu_custom_call" | custom-call | tf_op jit(solution)/shard_map/pallas_call | solution.py:503

commit v6 on v5

--- a/solution.py
+++ b/solution.py
@@ -13,9 +13,9 @@
 CUT = 40
 PASS = (0, 3, 4, 7, 1, 2, 5, 6)
 ORDER = tuple(4 * (j // 2) + j % 2 + 2 * way for j in PASS for way in range(2))
-TURNS = (1, 4, 8)
+TURNS = (3, 9, 15, 21)
 EARLY = 4
-WHEN = (24, 30, 36, 42, 50, 55, 60, 65, 70, 75, 80, 85, 90, 95, 100, 105, 110, 115, 120, 125)
+WHEN = (12, 18, 24, 30, 50, 55, 60, 65, 70, 75, 80, 85, 90, 95, 100, 105, 110, 115, 120, 125)
 STRIDE = (16, 4, 1)
 F32 = jnp.float32
 
@@ -98,13 +98,14 @@
 
 def kernel(
     weight_ref, count_ref, list_ref, strip_ref, tile_ref, factor_ref, inverse_ref, sum_ref,
-    strip, scaled, tile, left, lives, slots, table, acc,
+    strip, scaled, tile0, tile1, left, lives, slots, table, acc,
     fwd1, fin1, fwd2, fin2, fwd3, fin3,
     diagonal_ref, dfull, dx, dquarter, dy, dz, dquarter2,
     load_sem, sib_send, sib_recv,
     fwd1_recv, fin1_recv, fwd2_recv, fin2_recv, out_send, last_recv,
     d_send, d_recv,
 ):
+    tile = (tile0, tile1)
     row, col = lax.axis_index("row"), lax.axis_index("col")
     core = lax.rem(row, 2)
     place = (lax.div(row, 2), lax.div(col, 4), lax.rem(col, 4))
@@ -132,9 +133,15 @@
     for partner in partners:
         pl.semaphore_signal(barrier, inc=1, device_id=partner, device_id_type=MESH)
     get_strip = pltpu.make_async_copy(strip_ref, strip.at[pl.ds(0, blocks)], load_sem.at[0])
-    get_tile = pltpu.make_async_copy(tile_ref, tile.at[pl.ds(0, items)], load_sem.at[1])
+    get_tile = [
+        pltpu.make_async_copy(
+            tile_ref.at[:, :, pl.ds(128 * h, 128)], tile[h].at[pl.ds(0, items)], load_sem.at[(1, 4)[h]]
+        )
+        for h in range(2)
+    ]
     get_strip.start()
-    get_tile.start()
+    for copy in get_tile:
+        copy.start()
 
     lane = lax.broadcasted_iota(jnp.int32, (blocks, 128), 1)
     block = lax.broadcasted_iota(jnp.int32, (blocks, 128), 0)
@@ -187,7 +194,10 @@
             (lives.at[0], lives.at[1]),
             (strip_ref, strip.at[pl.ds(blocks, blocks)]),
             (slots.at[0], slots.at[1]),
-            (tile_ref, tile.at[pl.ds(items, items)]),
+            *[
+                (tile_ref.at[:, :, pl.ds(128 * h, 128)], tile[h].at[pl.ds(items, items)])
+                for h in range(2)
+            ],
         ])
     ]
     for copy in across:
@@ -199,13 +209,13 @@
     weigh(0)
     build(0, 0)
 
-    def product(ty, tx, tz):
+    def product(h, ty, tx, tz):
         number = ((ty * 2 + core) * 4 + tx) * 4 + tz
         lefts, rights = [], []
         for n in range(4):
             slot = table[n // 2, n % 2, number]
             lefts.append(left[lax.div(slot, 4) + (n // 2) * (blocks + 1)])
-            high, low = split(tile[lax.rem(slot, items) + (n // 2) * items])
+            high, low = split(tile[h][lax.rem(slot, items) + (n // 2) * items])
             rights += [high, low, high, low]
         return dot(jnp.concatenate(lefts, axis=1), jnp.concatenate(rights, axis=0))
 
@@ -220,17 +230,17 @@
     def rows_of(p):
         return pl.ds(*ROWS[p])
 
-    def fwd_copy(stage, p, way, k, j):
+    def fwd_copy(stage, p, way, k, j, columns=pl.ds(0, 256)):
         fwd, recv = ((fwd1, fwd1_recv), (fwd2, fwd2_recv))[stage - 1]
         return remote(
-            acc.at[k, rows_of(p)], fwd.at[way, j, rows_of(p)],
+            acc.at[k, rows_of(p), columns], fwd.at[way, j, rows_of(p), columns],
             out_send.at[2 * stage - 2], recv.at[j], peer((p + stage - 1) % 3, 1 + 2 * way),
         )
 
-    def fin_copy(stage, p, way, k, j):
+    def fin_copy(stage, p, way, k, j, columns=pl.ds(0, 256)):
         fin, recv = ((fin1, fin1_recv), (fin2, fin2_recv))[stage - 1]
         return remote(
-            acc.at[k, rows_of(p)], fin.at[way, j, rows_of(p)],
+            acc.at[k, rows_of(p), columns], fin.at[way, j, rows_of(p), columns],
             out_send.at[2 * stage - 1], recv.at[j], peer((p + stage - 1) % 3, 1 + 2 * way),
         )
 
@@ -240,7 +250,7 @@
     def all_gone(buffer, send):
         remote(buffer, buffer, send, last_recv.at[0], sibling).wait_send()
 
-    def send_on(k, digit):
+    def send_on(k, digit, columns):
         for p in range(3):
             da, db, dc = digit[p], digit[(p + 1) % 3], digit[(p + 2) % 3]
 
@@ -250,24 +260,28 @@
             @pl.when(da == 0)
             def _():
                 way = jnp.where(dc < 2, 0, 1)
-                fwd_copy(1, p, way, k, db * 2 + lax.rem(dc, 2)).start()
+                fwd_copy(1, p, way, k, db * 2 + lax.rem(dc, 2), columns).start()
 
             @pl.when(((da == 1) & (dc >= 2)) | ((da == 2) & (dc < 2)))
             def _():
-                fin_copy(1, p, da - 1, k, db * 4 + dc).start()
-
-    def tiles(i, carry):
+                fin_copy(1, p, da - 1, k, db * 4 + dc, columns).start()
+
+    def tiles(half, i, carry):
+        columns = pl.ds(128 * half, 128)
         group = group_digits(i)
         at = [y * 16 + x * 4 + z for y, x, z in group]
         for k, digit in zip(at, group):
-            acc[k] = product(*[lax.rem(place[a] + offset(digit[a]), 4) for a in range(3)])
+            acc[k, :, columns] = product(half, *[lax.rem(place[a] + offset(digit[a]), 4) for a in range(3)])
         for k, digit in zip(at, group):
-            send_on(k, digit)
+            send_on(k, digit, columns)
         for phase, after in enumerate(TURNS):
-            @pl.when(i == after)
+            if after // 16 != half:
+                continue
+
+            @pl.when(i == after % 16)
             def _():
-                d_arrive(phase + 1)
-                d_start(phase + 2)
+                d_arrive(phase)
+                d_start(phase + 1)
 
         return carry
 
@@ -338,13 +352,14 @@
     across[2].wait_recv()
     their_table = pltpu.make_async_copy(slots.at[1], table.at[1], load_sem.at[3])
     their_table.start()
-    d_arrive(0)
-    d_start(1)
     own_table.wait()
     their_table.wait()
-    get_tile.wait()
+    for copy in get_tile:
+        copy.wait()
     across[3].wait_recv()
-    lax.fori_loop(0, 16, tiles, 0)
+    lax.fori_loop(0, 16, functools.partial(tiles, 0), 0)
+    across[4].wait_recv()
+    lax.fori_loop(0, 16, functools.partial(tiles, 1), 0)
 
     def slot(p, da, db, dc):
         digit = [0, 0, 0]
@@ -428,8 +443,10 @@
         sum_ref[...] = acc[63] + fin3[0] + fin3[1]
 
     events = [functools.partial(pass1, j) for j in PASS]
-    events += [functools.partial(gather1, f) for f in ORDER]
-    events += [functools.partial(pass2, j) for j in range(2)]
+    events += [functools.partial(gather1, f) for f in ORDER[:14]]
+    events += [functools.partial(pass2, 0)]
+    events += [functools.partial(gather1, f) for f in ORDER[14:]]
+    events += [functools.partial(pass2, 1)]
     events += [functools.partial(gather2, dc) for dc in range(4)]
     events += [pass3, gather3]
     for event in events[:EARLY]:
@@ -471,7 +488,7 @@
         out_specs=[in_vmem] * 3,
         scratch_shapes=[
             vmem(2 * blocks, width, rows), vmem(2 * blocks, width, rows),
-            vmem(2 * items, width, rows),
+            vmem(2 * items, width, 128), vmem(2 * items, width, 128),
             pltpu.VMEM((2 * blocks + 2, rows, 4 * width), jnp.bfloat16),
             vmem(2, width, 128), pltpu.VMEM((2, 2, 128), jnp.int32), pltpu.SMEM((2, 2, 128), jnp.int32),
             vmem(64, 256, 256),
@@ -480,7 +497,7 @@
             vmem(256, 256),
             vmem(256, 256), vmem(7, 32, 256), vmem(32, 256),
             vmem(3, 8, 256), vmem(4, 8, 256), vmem(32, 256),
-            dma((4,)), dma((4,)), dma((4,)),
+            dma((5,)), dma((5,)), dma((5,)),
             dma((8,)), dma((16,)), dma((2,)), dma((4,)), dma((6,)), dma((2,)),
             dma((5,)), dma((5,)),
         ],

time: 89.3 us -> 85.6 us (0.959)
  Pallas kernels: 88.4 us -> 84.8 us
    pallas_call x1, Pallas kernels: 86.2 us -> 82.5 us  [gather_and_sum(): pl.pallas_call(kernel, out_shape=[jax.ShapeDtypeStruct((256, 256), F32)]...]
where the time goes in v6:
time: 85.6 us; the launch traced here: 85.4 us
  Pallas kernels  84.8 us (99%)
    pallas_call x1, Pallas kernels, gather_and_sum(): pl.pallas_call(kernel, out_shape=[jax.ShapeDtypeStruct((256, 256), F32)]...  82.5 us
    pallas_call x1, Pallas kernels, per_device(): pl.pallas_call(finish, out_shape=[jax.ShapeDtypeStruct((256, 256), F32)]...  2.22 us

profile of v6, /device:TPU:0, one launch (start us, length us, event | category | flops | bytes accessed | tf_op | source)
XLA Modules:
  0.0 85.4 jit_solution(7265625858102725172)
XLA Ops:
  0.6 82.5 %shard_map.68 = (f32[256,256]{1,0:T(8,128)}, f32[256,256]{1,0:T(8,128)}, f32[256,256]{1,0:T(8,128)}) custom-call(f32[32,32]{1,0:T(8,128)} %weight_ref.1, s32[1,32]{1,0:T(1,128)} %bitcast.5, s32[4,32]{1,0:T(4,128)} %bitcast.4, f32[32,32,256]{2,1,0:T(8,128)} %strip_ref.1, f32[128,32,256]{2,1,0:T(8,128)} %bitcast.3), custom_call_target="tpu_custom_call" | custom-call | tf_op jit(solution)/shard_map/pallas_call | solution.py:484
  83.2 2.2 %shard_map.69 = (f32[256,256]{1,0:T(8,128)}, f32[256,256]{1,0:T(8,128)}) custom-call(f32[256,256]{1,0:T(8,128)} %get-tuple-element.5.factor_ref, f32[256,256]{1,0:T(8,128)} %get-tuple-element.6.inverse_ref, f32[256,256]{1,0:T(8,128)} %get-tuple-element.7.sum_ref), custom_call_target="tpu_custom_call" | custom-call | tf_op jit(solution)/shard_map/pallas_call | solution.py:520
